TPU v7x, 512 devices: a whole 4x4x16 slice. The times are simulated.
512 devices in a mesh: lat: 32 (over z, x_lo), lon: 16 (over y, x_hi, core).
Axes of the slice: x: 4 (x_hi: 2, x_lo: 2; x = x_hi * 2 + x_lo), y: 4, z: 16, core: 2. Of those that a mesh axis runs over, the one named last changes fastest.
Arguments:
- observed: float32 [4096, 8192], P(('lat', 'lon')), may hold values from -12 to 12
- gauged: int32 [4096, 8192], P('lat', 'lon'), may hold values from 0 to 1, as said below
Outputs:
- coarsest_coeffs: float32 [512, 1024], P('lat', 'lon')
- coarse_coeffs: float32 [1024, 2048], P('lat', 'lon')
- fine_coeffs: float32 [2048, 4096], P('lat', 'lon')
- finest_coeffs: float32 [4096, 8192], P('lat', 'lon')
- imputed: float32 [4096, 8192], P(('lat', 'lon'))
Inputs may be any that keep to these rules, and one draw needn't show every extreme that they name: 1 marks a gauged cell.
All inputs are finite; a program needn't handle non-finite values.
Results may differ from a plain program's by a relative error of at most 0.00029.
Values sent between devices are 32-bit elements; how exact they have to be, the bound alone decides.
A program may use at most 64 MiB of HBM per device.

v0:
```python
import math

import jax
import jax.numpy as jnp
from jax import lax
from jax.sharding import PartitionSpec as P

LEVELS = 4
ITERS = 2


highest = lax.Precision.HIGHEST
data_weight = 2.0
kappa_term = 5.0
level_scales = (0.02, 0.03, 0.05, 0.08)


def with_halo(x, sides, width):
    for axis, dim in sides:
        size, length = (lax.axis_size(axis), x.shape[dim])
        up = [(i, (i + 1) % size) for i in range(size - 1)]
        down = [(j, i) for i, j in up]
        last = lax.slice_in_dim(x, length - width, length, axis=dim)
        first = lax.slice_in_dim(x, 0, width, axis=dim)
        before = lax.ppermute(last, axis, up)
        after = lax.ppermute(first, axis, down)
        x = jnp.concatenate([before, x, after], axis=dim)
    return x


def wendland(distance):
    remain = jnp.maximum(1.0 - distance, 0.0)
    return remain**6 * (35.0 * distance * distance + 18.0 * distance + 3.0) / 3.0


def basis_table(cell_total, node_total, spacing, cell_margin, node_margin):
    shape_full = (cell_total + 2 * cell_margin, node_total + 2 * node_margin)
    cell_idx = lax.broadcasted_iota(jnp.int32, shape_full, 0) - cell_margin
    node_idx = lax.broadcasted_iota(jnp.int32, shape_full, 1) - node_margin
    numerator = jnp.abs(2 * cell_idx - 2 * spacing * node_idx - (spacing - 1))
    return wendland(numerator.astype(jnp.float32) / (5.0 * spacing)) / math.sqrt(spacing)


def matmul(left, right):
    return jnp.dot(left, right, precision=highest, preferred_element_type=jnp.float32)


def stencil(values):
    beside = values[2:, 1:-1] + values[:-2, 1:-1] + values[1:-1, 2:] + values[1:-1, :-2]
    return kappa_term * values[1:-1, 1:-1] - beside


def level_products(first, second):
    accum = jnp.float32(0.0)
    for level_idx in range(len(first)):
        accum = accum + jnp.sum(first[level_idx] * second[level_idx])
    return accum


def norm_sum(residual):
    return lax.psum(level_products(residual, residual), ("lat", "lon"))


def body(observed, gauged):
    tiled = lax.all_to_all(observed, "lon", split_axis=1, concat_axis=0, tiled=True)
    lat_index = lax.axis_index("lat")
    lon_index = lax.axis_index("lon")
    lat_total = lax.axis_size("lat")
    lon_total = lax.axis_size("lon")
    rows_here, cols_here = gauged.shape
    gauge_float = gauged.astype(jnp.float32)
    spacings = [2 ** (LEVELS - 1 - level_idx) for level_idx in range(LEVELS)]
    node_shapes = [(rows_here // sp, cols_here // sp) for sp in spacings]
    fwd_lat = [basis_table(rows_here, node_shapes[k][0], spacings[k], 0, 2) for k in range(LEVELS)]
    fwd_lon = [basis_table(cols_here, node_shapes[k][1], spacings[k], 0, 2) for k in range(LEVELS)]
    valid_nodes = []
    for k in range(LEVELS):
        node_rows, node_cols = node_shapes[k]
        row_global = (
            lat_index * node_rows + lax.broadcasted_iota(jnp.int32, (node_rows + 2, 1), 0) - 1
        )
        col_global = (
            lon_index * node_cols + lax.broadcasted_iota(jnp.int32, (1, node_cols + 2), 1) - 1
        )
        row_valid = (row_global >= 0) & (row_global < node_rows * lat_total)
        col_valid = (col_global >= 0) & (col_global < node_cols * lon_total)
        valid_nodes.append((row_valid & col_valid).astype(jnp.float32))

    def synthesize(coeffs):
        surface = jnp.zeros((rows_here, cols_here), jnp.float32)
        extended_all = []
        for k in range(LEVELS):
            extended = with_halo(coeffs[k], (("lat", 0), ("lon", 1)), 2)
            surface = surface + matmul(matmul(fwd_lat[k], extended), fwd_lon[k].T)
            extended_all.append(extended)
        return (surface, extended_all)

    def adjoint(misfit):
        result = []
        widened = with_halo(misfit, (("lat", 0), ("lon", 1)), 16)
        for k in range(LEVELS):
            back_lat = basis_table(rows_here, node_shapes[k][0], spacings[k], 16, 0).T
            back_lon = basis_table(cols_here, node_shapes[k][1], spacings[k], 16, 0)
            result.append(matmul(matmul(back_lat, widened), back_lon))
        return result

    right_side = adjoint(data_weight * gauge_float * tiled)
    solution = [jnp.zeros_like(piece) for piece in right_side]
    surface_sum = jnp.zeros((rows_here, cols_here), jnp.float32)
    residual = right_side
    search = right_side
    res_norm = norm_sum(residual)
    for iteration in range(ITERS):
        apply_surface, apply_extended_all = synthesize(search)
        backs = adjoint(data_weight * gauge_float * apply_surface)
        curv_local = data_weight * jnp.sum(gauge_float * apply_surface * apply_surface)
        images = []
        for apply_k in range(LEVELS):
            smoothed = stencil(apply_extended_all[apply_k]) * valid_nodes[apply_k]
            images.append(backs[apply_k] + level_scales[apply_k] * stencil(smoothed))
            own_part = smoothed[1:-1, 1:-1]
            curv_local = curv_local + level_scales[apply_k] * jnp.sum(own_part * own_part)
        images, surface, curv_local = (images, apply_surface, curv_local)
        curv_sum = lax.psum(curv_local, ("lat", "lon"))
        step_size = res_norm / curv_sum
        solution = [solution[k] + step_size * search[k] for k in range(LEVELS)]
        surface_sum = surface_sum + step_size * surface
        if iteration + 1 < ITERS:
            residual = [residual[k] - step_size * images[k] for k in range(LEVELS)]
            new_norm = norm_sum(residual)
            search = [residual[k] + new_norm / res_norm * search[k] for k in range(LEVELS)]
            res_norm = new_norm
    final_surface, unused_rims = synthesize(solution)
    swath_field = lax.all_to_all(final_surface, "lon", split_axis=0, concat_axis=1, tiled=True)
    return (solution[0], solution[1], solution[2], solution[3], swath_field)


def solution(mesh):
    placed = (P(("lat", "lon"), None), P("lat", "lon"))
    return jax.shard_map(
        body,
        mesh=mesh,
        in_specs=placed,
        out_specs=(
            P("lat", "lon"),
            P("lat", "lon"),
            P("lat", "lon"),
            P("lat", "lon"),
            P(("lat", "lon"), None),
        ),
        check_vma=False,
    )
```

profile of v0, /device:TPU:1, one launch (start us, length us, event | category | flops | bytes accessed | tf_op | source)
XLA Modules:
  0.0 622.4 jit_solution(1043832198746908045)
XLA Ops:
  0.6 10.3 %all-to-all-start = ((f32[8,16,512]{2,0,1:T(8,128)}), f32[8,16,512]{2,0,1:T(8,128)S(1)}, u32[]{:S(2)}, u32[]{:S(2)}) async-start(f32[8,16,512]{2,0,1:T(8,128)} %bitcast.39), calls=%async_computation | async-start | bytes 524288 | tf_op jit(solution)/shard_map/all_to_all | solution.py:65
  11.5 8.3 %all-to-all-done = f32[8,16,512]{2,0,1:T(8,128)S(1)} async-done(((f32[8,16,512]{2,0,1:T(8,128)}), f32[8,16,512]{2,0,1:T(8,128)S(1)}, u32[]{:S(2)}, u32[]{:S(2)}) %all-to-all-start) | async-done | bytes 262176 | tf_op jit(solution)/shard_map/all_to_all | solution.py:65
  21.1 4.0 collective-permute-start
  26.2 4.0 collective-permute-start.3
  30.2 3.1 collective-permute-start.2
  37.5 4.3 collective-permute-start.4
  45.1 4.9 collective-permute-start.12
  53.7 2.3 multiply_reduce_fusion.2
  58.0 7.2 %collective-permute-start.6 = (f32[20,2]{1,0:T(8,128)S(1)}, f32[20,2]{1,0:T(8,128)S(1)}, u32[]{:S(2)}, u32[]{:S(2)}) collective-permute-start(f32[20,2]{1,0:T(8,128)S(1)} %get-tuple-element.69), channel_id=1, source_target_pairs={{0,1},{1,2},{2,3},{3,4},{4,5},{5,6},{6,7},{7,8},{8,9},{9,10},{10,1... | collective-permute-start | bytes 488 | tf_op jit(solution)/shard_map/ppermute | solution.py:25
  65.9 1.9 collective-permute-start.7
  67.8 4.6 collective-permute-start.8
  77.6 6.0 collective-permute-start.10
  84.3 4.9 collective-permute-start.16
  89.9 1.9 collective-permute-start.15
  91.8 5.1 collective-permute-start.14
  101.7 1.9 collective-permute-start.19
  103.6 5.9 collective-permute-start.18
  111.7 2.8 fusion.106
  115.7 5.4 collective-permute-start.20
  123.9 1.9 collective-permute-start.23
  125.8 6.2 collective-permute-start.22
  132.1 117.3 %all-reduce = (f32[]{:T(128)}, f32[]{:T(128)}) all-reduce(f32[]{:T(128)S(6)} %add.627, f32[]{:T(128)S(6)} %add.678), channel_id=1, replica_groups=mesh['lat'=32,'lon'=16] {'lat','lon'}, use_global_device_ids=true, to_apply=%region_4.0 | all-reduce | flops 2 | bytes 16 | tf_op jit(solution)/shard_map/psum | solution.py:61
  256.6 2.3 multiply_reduce_fusion
  261.7 100.0 %psum.30 = f32[]{:T(128)} all-reduce(f32[]{:T(128)S(6)} %add.697), channel_id=1, replica_groups=mesh['lat'=32,'lon'=16] {'lat','lon'}, use_global_device_ids=true, to_apply=%region_15.0 | all-reduce | flops 1 | bytes 8 | tf_op jit(solution)/shard_map/psum | solution.py:61
  364.3 4.0 collective-permute-start.32
  369.6 4.0 collective-permute-start.24
  375.1 3.7 collective-permute-start.27
  378.8 3.9 collective-permute-start.26
  382.8 4.6 collective-permute-start.28
  391.8 5.3 collective-permute-start.30
  398.5 5.8 collective-permute-start.36
  406.9 5.1 collective-permute-start.34
  416.7 1.9 collective-permute-start.39
  418.7 5.4 collective-permute-start.38
  426.7 2.8 fusion.48
  431.9 108.5 %psum.31 = f32[]{:T(128)} all-reduce(f32[]{:T(128)S(6)} %add.720), channel_id=1, replica_groups=mesh['lat'=32,'lon'=16] {'lat','lon'}, use_global_device_ids=true, to_apply=%region_21.0 | all-reduce | flops 1 | bytes 8 | tf_op jit(solution)/shard_map/psum | solution.py:124
  543.2 4.0 collective-permute-start.48
  548.5 4.7 collective-permute-start.40
  554.7 3.4 collective-permute-start.43
  558.1 4.2 collective-permute-start.42
  562.3 4.6 collective-permute-start.44
  569.2 5.8 collective-permute-start.52
  577.0 5.1 collective-permute-start.46
  584.2 5.1 collective-permute-start.50
  592.4 1.9 collective-permute-start.55
  594.3 5.9 collective-permute-start.54
  602.1 2.2 fusion.7
  604.3 17.1 %all_to_all.38 = f32[16,8,512]{2,1,0:T(8,128)S(1)} all-to-all(f32[16,8,512]{2,1,0:T(8,128)S(1)} %fusion.7), channel_id=1, replica_groups=mesh['lat'=32,'lon'=16] {'lon'}, dimensions={0} | all-to-all | bytes 524288 | tf_op jit(solution)/shard_map/all_to_all | solution.py:134
  (221 shorter events, 68.5 us)
Async XLA Ops:
  0.6 19.1 %all-to-all-start = ((f32[8,16,512]{2,0,1:T(8,128)}), f32[8,16,512]{2,0,1:T(8,128)S(1)}, u32[]{:S(2)}, u32[]{:S(2)}) async-start(f32[8,16,512]{2,0,1:T(8,128)} %bitcast.39), calls=%async_computation | async-start | bytes 524288 | tf_op jit(solution)/shard_map/all_to_all | solution.py:65
  26.2 7.3 %collective-permute-start.3 = (f32[160,16]{1,0:T(8,128)S(1)}, f32[160,16]{1,0:T(8,128)S(1)}, u32[]{:S(2)}, u32[]{:S(2)}) collective-permute-start(f32[160,16]{1,0:T(8,128)S(1)} %get-tuple-element.15), channel_id=1, source_target_pairs={{1,0},{2,1},{3,2},{4,3},{5,4},{6,5},{7,6},{8,7},{9,8},{10,9},{11,1... | collective-permute-start | bytes 30728 | tf_op jit(solution)/shard_map/ppermute | solution.py:26
  36.2 21.7 %collective-permute-start.5 = (f32[2,64]{1,0:T(2,128)S(1)}, f32[2,64]{1,0:T(2,128)S(1)}, u32[]{:S(2)}, u32[]{:S(2)}) collective-permute-start(f32[2,64]{1,0:T(2,128)S(1)} %get-tuple-element.76), channel_id=1, source_target_pairs={{16,0},{32,16},{48,32},{64,48},{80,64},{96,80},{112,96},{128,112},... | collective-permute-start | bytes 1544 | tf_op jit(solution)/shard_map/ppermute | solution.py:26
  37.5 20.4 %collective-permute-start.4 = (f32[2,64]{1,0:T(2,128)S(1)}, f32[2,64]{1,0:T(2,128)S(1)}, u32[]{:S(2)}, u32[]{:S(2)}) collective-permute-start(f32[2,64]{1,0:T(2,128)S(1)} %get-tuple-element.75), channel_id=1, source_target_pairs={{0,16},{16,32},{32,48},{48,64},{64,80},{80,96},{96,112},{112,128},... | collective-permute-start | bytes 1544 | tf_op jit(solution)/shard_map/ppermute | solution.py:25
  43.9 45.9 %collective-permute-start.13 = (f32[2,256]{1,0:T(2,128)S(1)}, f32[2,256]{1,0:T(2,128)S(1)}, u32[]{:S(2)}, u32[]{:S(2)}) collective-permute-start(f32[2,256]{1,0:T(2,128)S(1)} %get-tuple-element.46), channel_id=1, source_target_pairs={{16,0},{32,16},{48,32},{64,48},{80,64},{96,80},{112,96},{128,112},... | collective-permute-start | bytes 6152 | tf_op jit(solution)/shard_map/ppermute | solution.py:26
  45.1 44.7 %collective-permute-start.12 = (f32[2,256]{1,0:T(2,128)S(1)}, f32[2,256]{1,0:T(2,128)S(1)}, u32[]{:S(2)}, u32[]{:S(2)}) collective-permute-start(f32[2,256]{1,0:T(2,128)S(1)} %get-tuple-element.45), channel_id=1, source_target_pairs={{0,16},{16,32},{32,48},{48,64},{64,80},{80,96},{96,112},{112,128},... | collective-permute-start | bytes 6152 | tf_op jit(solution)/shard_map/ppermute | solution.py:25
  51.7 23.2 %collective-permute-start.9 = (f32[2,128]{1,0:T(2,128)S(1)}, f32[2,128]{1,0:T(2,128)S(1)}, u32[]{:S(2)}, u32[]{:S(2)}) collective-permute-start(f32[2,128]{1,0:T(2,128)S(1)} %get-tuple-element.61), channel_id=1, source_target_pairs={{16,0},{32,16},{48,32},{64,48},{80,64},{96,80},{112,96},{128,112},... | collective-permute-start | bytes 3080 | tf_op jit(solution)/shard_map/ppermute | solution.py:26
  58.0 9.8 %collective-permute-start.6 = (f32[20,2]{1,0:T(8,128)S(1)}, f32[20,2]{1,0:T(8,128)S(1)}, u32[]{:S(2)}, u32[]{:S(2)}) collective-permute-start(f32[20,2]{1,0:T(8,128)S(1)} %get-tuple-element.69), channel_id=1, source_target_pairs={{0,1},{1,2},{2,3},{3,4},{4,5},{5,6},{6,7},{7,8},{8,9},{9,10},{10,1... | collective-permute-start | bytes 488 | tf_op jit(solution)/shard_map/ppermute | solution.py:25
  67.8 7.1 %collective-permute-start.8 = (f32[2,128]{1,0:T(2,128)S(1)}, f32[2,128]{1,0:T(2,128)S(1)}, u32[]{:S(2)}, u32[]{:S(2)}) collective-permute-start(f32[2,128]{1,0:T(2,128)S(1)} %get-tuple-element.60), channel_id=1, source_target_pairs={{0,16},{16,32},{32,48},{48,64},{64,80},{80,96},{96,112},{112,128},... | collective-permute-start | bytes 3080 | tf_op jit(solution)/shard_map/ppermute | solution.py:25
  72.4 29.2 %collective-permute-start.17 = (f32[2,512]{1,0:T(2,128)S(1)}, f32[2,512]{1,0:T(2,128)S(1)}, u32[]{:S(2)}, u32[]{:S(2)}) collective-permute-start(f32[2,512]{1,0:T(2,128)S(1)} %get-tuple-element.29), channel_id=1, source_target_pairs={{16,0},{32,16},{48,32},{64,48},{80,64},{96,80},{112,96},{128,112},... | collective-permute-start | bytes 12296 | tf_op jit(solution)/shard_map/ppermute | solution.py:26
  75.0 9.3 %collective-permute-start.11 = (f32[36,2]{1,0:T(8,128)S(1)}, f32[36,2]{1,0:T(8,128)S(1)}, u32[]{:S(2)}, u32[]{:S(2)}) collective-permute-start(f32[36,2]{1,0:T(8,128)S(1)} %get-tuple-element.55), channel_id=1, source_target_pairs={{1,0},{2,1},{3,2},{4,3},{5,4},{6,5},{7,6},{8,7},{9,8},{10,9},{11,1... | collective-permute-start | bytes 872 | tf_op jit(solution)/shard_map/ppermute | solution.py:26
  77.6 11.6 %collective-permute-start.10 = (f32[36,2]{1,0:T(8,128)S(1)}, f32[36,2]{1,0:T(8,128)S(1)}, u32[]{:S(2)}, u32[]{:S(2)}) collective-permute-start(f32[36,2]{1,0:T(8,128)S(1)} %get-tuple-element.54), channel_id=1, source_target_pairs={{0,1},{1,2},{2,3},{3,4},{4,5},{5,6},{6,7},{7,8},{8,9},{9,10},{10,1... | collective-permute-start | bytes 872 | tf_op jit(solution)/shard_map/ppermute | solution.py:25
  84.3 17.3 %collective-permute-start.16 = (f32[2,512]{1,0:T(2,128)S(1)}, f32[2,512]{1,0:T(2,128)S(1)}, u32[]{:S(2)}, u32[]{:S(2)}) collective-permute-start(f32[2,512]{1,0:T(2,128)S(1)} %get-tuple-element.28), channel_id=1, source_target_pairs={{0,16},{16,32},{32,48},{48,64},{64,80},{80,96},{96,112},{112,128},... | collective-permute-start | bytes 12296 | tf_op jit(solution)/shard_map/ppermute | solution.py:25
  89.9 8.4 %collective-permute-start.15 = (f32[68,2]{1,0:T(8,128)S(1)}, f32[68,2]{1,0:T(8,128)S(1)}, u32[]{:S(2)}, u32[]{:S(2)}) collective-permute-start(f32[68,2]{1,0:T(8,128)S(1)} %get-tuple-element.40), channel_id=1, source_target_pairs={{1,0},{2,1},{3,2},{4,3},{5,4},{6,5},{7,6},{8,7},{9,8},{10,9},{11,1... | collective-permute-start | bytes 1640 | tf_op jit(solution)/shard_map/ppermute | solution.py:26
  101.7 9.2 %collective-permute-start.19 = (f32[132,2]{1,0:T(8,128)S(1)}, f32[132,2]{1,0:T(8,128)S(1)}, u32[]{:S(2)}, u32[]{:S(2)}) collective-permute-start(f32[132,2]{1,0:T(8,128)S(1)} %get-tuple-element.21), channel_id=1, source_target_pairs={{1,0},{2,1},{3,2},{4,3},{5,4},{6,5},{7,6},{8,7},{9,8},{10,9},{11,1... | collective-permute-start | bytes 3176 | tf_op jit(solution)/shard_map/ppermute | solution.py:26
  103.6 7.2 %collective-permute-start.18 = (f32[132,2]{1,0:T(8,128)S(1)}, f32[132,2]{1,0:T(8,128)S(1)}, u32[]{:S(2)}, u32[]{:S(2)}) collective-permute-start(f32[132,2]{1,0:T(8,128)S(1)} %get-tuple-element.20), channel_id=1, source_target_pairs={{0,1},{1,2},{2,3},{3,4},{4,5},{5,6},{6,7},{7,8},{8,9},{9,10},{10,1... | collective-permute-start | bytes 3176 | tf_op jit(solution)/shard_map/ppermute | solution.py:25
  114.5 9.3 %collective-permute-start.21 = (f32[16,512]{1,0:T(8,128)S(1)}, f32[16,512]{1,0:T(8,128)S(1)}, u32[]{:S(2)}, u32[]{:S(2)}) collective-permute-start(f32[16,512]{1,0:T(8,128)S(1)} %get-tuple-element.27), channel_id=1, source_target_pairs={{16,0},{32,16},{48,32},{64,48},{80,64},{96,80},{112,96},{128,112},... | collective-permute-start | bytes 98312 | tf_op jit(solution)/shard_map/ppermute | solution.py:26
  115.7 8.0 %collective-permute-start.20 = (f32[16,512]{1,0:T(8,128)S(1)}, f32[16,512]{1,0:T(8,128)S(1)}, u32[]{:S(2)}, u32[]{:S(2)}) collective-permute-start(f32[16,512]{1,0:T(8,128)S(1)} %get-tuple-element.26), channel_id=1, source_target_pairs={{0,16},{16,32},{32,48},{48,64},{64,80},{80,96},{96,112},{112,128},... | collective-permute-start | bytes 98312 | tf_op jit(solution)/shard_map/ppermute | solution.py:25
  123.9 126.8 %collective-permute-start.23 = (f32[160,16]{1,0:T(8,128)S(1)}, f32[160,16]{1,0:T(8,128)S(1)}, u32[]{:S(2)}, u32[]{:S(2)}) collective-permute-start(f32[160,16]{1,0:T(8,128)S(1)} %get-tuple-element.13), channel_id=1, source_target_pairs={{1,0},{2,1},{3,2},{4,3},{5,4},{6,5},{7,6},{8,7},{9,8},{10,9},{11,1... | collective-permute-start | bytes 30728 | tf_op jit(solution)/shard_map/ppermute | solution.py:26
  125.8 124.9 %collective-permute-start.22 = (f32[160,16]{1,0:T(8,128)S(1)}, f32[160,16]{1,0:T(8,128)S(1)}, u32[]{:S(2)}, u32[]{:S(2)}) collective-permute-start(f32[160,16]{1,0:T(8,128)S(1)} %get-tuple-element.12), channel_id=1, source_target_pairs={{0,1},{1,2},{2,3},{3,4},{4,5},{5,6},{6,7},{7,8},{8,9},{9,10},{10,1... | collective-permute-start | bytes 30728 | tf_op jit(solution)/shard_map/ppermute | solution.py:25
  363.0 41.9 %collective-permute-start.33 = (f32[2,256]{1,0:T(2,128)S(1)}, f32[2,256]{1,0:T(2,128)S(1)}, u32[]{:S(2)}, u32[]{:S(2)}) collective-permute-start(f32[2,256]{1,0:T(2,128)S(1)} %get-tuple-element.44), channel_id=1, source_target_pairs={{16,0},{32,16},{48,32},{64,48},{80,64},{96,80},{112,96},{128,112},... | collective-permute-start | bytes 6152 | tf_op jit(solution)/shard_map/ppermute | solution.py:26
  364.3 40.6 %collective-permute-start.32 = (f32[2,256]{1,0:T(2,128)S(1)}, f32[2,256]{1,0:T(2,128)S(1)}, u32[]{:S(2)}, u32[]{:S(2)}) collective-permute-start(f32[2,256]{1,0:T(2,128)S(1)} %get-tuple-element.43), channel_id=1, source_target_pairs={{0,16},{16,32},{32,48},{48,64},{64,80},{80,96},{96,112},{112,128},... | collective-permute-start | bytes 6152 | tf_op jit(solution)/shard_map/ppermute | solution.py:25
  368.3 6.7 %collective-permute-start.25 = (f32[2,64]{1,0:T(2,128)S(1)}, f32[2,64]{1,0:T(2,128)S(1)}, u32[]{:S(2)}, u32[]{:S(2)}) collective-permute-start(f32[2,64]{1,0:T(2,128)S(1)} %get-tuple-element.74), channel_id=1, source_target_pairs={{16,0},{32,16},{48,32},{64,48},{80,64},{96,80},{112,96},{128,112},... | collective-permute-start | bytes 1544 | tf_op jit(solution)/shard_map/ppermute | solution.py:26
  373.7 16.1 %collective-permute-start.29 = (f32[2,128]{1,0:T(2,128)S(1)}, f32[2,128]{1,0:T(2,128)S(1)}, u32[]{:S(2)}, u32[]{:S(2)}) collective-permute-start(f32[2,128]{1,0:T(2,128)S(1)} %get-tuple-element.59), channel_id=1, source_target_pairs={{16,0},{32,16},{48,32},{64,48},{80,64},{96,80},{112,96},{128,112},... | collective-permute-start | bytes 3080 | tf_op jit(solution)/shard_map/ppermute | solution.py:26
  375.1 7.6 %collective-permute-start.27 = (f32[20,2]{1,0:T(8,128)S(1)}, f32[20,2]{1,0:T(8,128)S(1)}, u32[]{:S(2)}, u32[]{:S(2)}) collective-permute-start(f32[20,2]{1,0:T(8,128)S(1)} %get-tuple-element.68), channel_id=1, source_target_pairs={{1,0},{2,1},{3,2},{4,3},{5,4},{6,5},{7,6},{8,7},{9,8},{10,9},{11,1... | collective-permute-start | bytes 488 | tf_op jit(solution)/shard_map/ppermute | solution.py:26
  378.8 8.5 %collective-permute-start.26 = (f32[20,2]{1,0:T(8,128)S(1)}, f32[20,2]{1,0:T(8,128)S(1)}, u32[]{:S(2)}, u32[]{:S(2)}) collective-permute-start(f32[20,2]{1,0:T(8,128)S(1)} %get-tuple-element.67), channel_id=1, source_target_pairs={{0,1},{1,2},{2,3},{3,4},{4,5},{5,6},{6,7},{7,8},{8,9},{9,10},{10,1... | collective-permute-start | bytes 488 | tf_op jit(solution)/shard_map/ppermute | solution.py:25
  382.8 7.0 %collective-permute-start.28 = (f32[2,128]{1,0:T(2,128)S(1)}, f32[2,128]{1,0:T(2,128)S(1)}, u32[]{:S(2)}, u32[]{:S(2)}) collective-permute-start(f32[2,128]{1,0:T(2,128)S(1)} %get-tuple-element.58), channel_id=1, source_target_pairs={{0,16},{16,32},{32,48},{48,64},{64,80},{80,96},{96,112},{112,128},... | collective-permute-start | bytes 3080 | tf_op jit(solution)/shard_map/ppermute | solution.py:25
  387.3 29.3 %collective-permute-start.37 = (f32[2,512]{1,0:T(2,128)S(1)}, f32[2,512]{1,0:T(2,128)S(1)}, u32[]{:S(2)}, u32[]{:S(2)}) collective-permute-start(f32[2,512]{1,0:T(2,128)S(1)} %get-tuple-element.25), channel_id=1, source_target_pairs={{16,0},{32,16},{48,32},{64,48},{80,64},{96,80},{112,96},{128,112},... | collective-permute-start | bytes 12296 | tf_op jit(solution)/shard_map/ppermute | solution.py:26
  389.9 8.6 %collective-permute-start.31 = (f32[36,2]{1,0:T(8,128)S(1)}, f32[36,2]{1,0:T(8,128)S(1)}, u32[]{:S(2)}, u32[]{:S(2)}) collective-permute-start(f32[36,2]{1,0:T(8,128)S(1)} %get-tuple-element.53), channel_id=1, source_target_pairs={{1,0},{2,1},{3,2},{4,3},{5,4},{6,5},{7,6},{8,7},{9,8},{10,9},{11,1... | collective-permute-start | bytes 872 | tf_op jit(solution)/shard_map/ppermute | solution.py:26
  391.8 12.5 %collective-permute-start.30 = (f32[36,2]{1,0:T(8,128)S(1)}, f32[36,2]{1,0:T(8,128)S(1)}, u32[]{:S(2)}, u32[]{:S(2)}) collective-permute-start(f32[36,2]{1,0:T(8,128)S(1)} %get-tuple-element.52), channel_id=1, source_target_pairs={{0,1},{1,2},{2,3},{3,4},{4,5},{5,6},{6,7},{7,8},{8,9},{9,10},{10,1... | collective-permute-start | bytes 872 | tf_op jit(solution)/shard_map/ppermute | solution.py:25
  398.5 18.1 %collective-permute-start.36 = (f32[2,512]{1,0:T(2,128)S(1)}, f32[2,512]{1,0:T(2,128)S(1)}, u32[]{:S(2)}, u32[]{:S(2)}) collective-permute-start(f32[2,512]{1,0:T(2,128)S(1)} %get-tuple-element.24), channel_id=1, source_target_pairs={{0,16},{16,32},{32,48},{48,64},{64,80},{80,96},{96,112},{112,128},... | collective-permute-start | bytes 12296 | tf_op jit(solution)/shard_map/ppermute | solution.py:25
  405.0 8.4 %collective-permute-start.35 = (f32[68,2]{1,0:T(8,128)S(1)}, f32[68,2]{1,0:T(8,128)S(1)}, u32[]{:S(2)}, u32[]{:S(2)}) collective-permute-start(f32[68,2]{1,0:T(8,128)S(1)} %get-tuple-element.38), channel_id=1, source_target_pairs={{1,0},{2,1},{3,2},{4,3},{5,4},{6,5},{7,6},{8,7},{9,8},{10,9},{11,1... | collective-permute-start | bytes 1640 | tf_op jit(solution)/shard_map/ppermute | solution.py:26
  416.7 8.8 %collective-permute-start.39 = (f32[132,2]{1,0:T(8,128)S(1)}, f32[132,2]{1,0:T(8,128)S(1)}, u32[]{:S(2)}, u32[]{:S(2)}) collective-permute-start(f32[132,2]{1,0:T(8,128)S(1)} %get-tuple-element.19), channel_id=1, source_target_pairs={{1,0},{2,1},{3,2},{4,3},{5,4},{6,5},{7,6},{8,7},{9,8},{10,9},{11,1... | collective-permute-start | bytes 3176 | tf_op jit(solution)/shard_map/ppermute | solution.py:26
  418.7 6.9 %collective-permute-start.38 = (f32[132,2]{1,0:T(8,128)S(1)}, f32[132,2]{1,0:T(8,128)S(1)}, u32[]{:S(2)}, u32[]{:S(2)}) collective-permute-start(f32[132,2]{1,0:T(8,128)S(1)} %get-tuple-element.18), channel_id=1, source_target_pairs={{0,1},{1,2},{2,3},{3,4},{4,5},{5,6},{6,7},{7,8},{8,9},{9,10},{10,1... | collective-permute-start | bytes 3176 | tf_op jit(solution)/shard_map/ppermute | solution.py:25
  541.9 35.1 %collective-permute-start.49 = (f32[2,256]{1,0:T(2,128)S(1)}, f32[2,256]{1,0:T(2,128)S(1)}, u32[]{:S(2)}, u32[]{:S(2)}) collective-permute-start(f32[2,256]{1,0:T(2,128)S(1)} %get-tuple-element.42), channel_id=1, source_target_pairs={{16,0},{32,16},{48,32},{64,48},{80,64},{96,80},{112,96},{128,112},... | collective-permute-start | bytes 6152 | tf_op jit(solution)/shard_map/ppermute | solution.py:26
  543.2 39.0 %collective-permute-start.48 = (f32[2,256]{1,0:T(2,128)S(1)}, f32[2,256]{1,0:T(2,128)S(1)}, u32[]{:S(2)}, u32[]{:S(2)}) collective-permute-start(f32[2,256]{1,0:T(2,128)S(1)} %get-tuple-element.41), channel_id=1, source_target_pairs={{0,16},{16,32},{32,48},{48,64},{64,80},{80,96},{96,112},{112,128},... | collective-permute-start | bytes 6152 | tf_op jit(solution)/shard_map/ppermute | solution.py:25
  547.2 7.4 %collective-permute-start.41 = (f32[2,64]{1,0:T(2,128)S(1)}, f32[2,64]{1,0:T(2,128)S(1)}, u32[]{:S(2)}, u32[]{:S(2)}) collective-permute-start(f32[2,64]{1,0:T(2,128)S(1)} %get-tuple-element.72), channel_id=1, source_target_pairs={{16,0},{32,16},{48,32},{64,48},{80,64},{96,80},{112,96},{128,112},... | collective-permute-start | bytes 1544 | tf_op jit(solution)/shard_map/ppermute | solution.py:26
  553.3 15.9 %collective-permute-start.45 = (f32[2,128]{1,0:T(2,128)S(1)}, f32[2,128]{1,0:T(2,128)S(1)}, u32[]{:S(2)}, u32[]{:S(2)}) collective-permute-start(f32[2,128]{1,0:T(2,128)S(1)} %get-tuple-element.57), channel_id=1, source_target_pairs={{16,0},{32,16},{48,32},{64,48},{80,64},{96,80},{112,96},{128,112},... | collective-permute-start | bytes 3080 | tf_op jit(solution)/shard_map/ppermute | solution.py:26
  554.7 7.6 %collective-permute-start.43 = (f32[20,2]{1,0:T(8,128)S(1)}, f32[20,2]{1,0:T(8,128)S(1)}, u32[]{:S(2)}, u32[]{:S(2)}) collective-permute-start(f32[20,2]{1,0:T(8,128)S(1)} %get-tuple-element.63), channel_id=1, source_target_pairs={{1,0},{2,1},{3,2},{4,3},{5,4},{6,5},{7,6},{8,7},{9,8},{10,9},{11,1... | collective-permute-start | bytes 488 | tf_op jit(solution)/shard_map/ppermute | solution.py:26
  558.1 8.8 %collective-permute-start.42 = (f32[20,2]{1,0:T(8,128)S(1)}, f32[20,2]{1,0:T(8,128)S(1)}, u32[]{:S(2)}, u32[]{:S(2)}) collective-permute-start(f32[20,2]{1,0:T(8,128)S(1)} %get-tuple-element.62), channel_id=1, source_target_pairs={{0,1},{1,2},{2,3},{3,4},{4,5},{5,6},{6,7},{7,8},{8,9},{9,10},{10,1... | collective-permute-start | bytes 488 | tf_op jit(solution)/shard_map/ppermute | solution.py:25
  562.3 12.7 %collective-permute-start.44 = (f32[2,128]{1,0:T(2,128)S(1)}, f32[2,128]{1,0:T(2,128)S(1)}, u32[]{:S(2)}, u32[]{:S(2)}) collective-permute-start(f32[2,128]{1,0:T(2,128)S(1)} %get-tuple-element.56), channel_id=1, source_target_pairs={{0,16},{16,32},{32,48},{48,64},{64,80},{80,96},{96,112},{112,128},... | collective-permute-start | bytes 3080 | tf_op jit(solution)/shard_map/ppermute | solution.py:25
  566.9 25.4 %collective-permute-start.53 = (f32[2,512]{1,0:T(2,128)S(1)}, f32[2,512]{1,0:T(2,128)S(1)}, u32[]{:S(2)}, u32[]{:S(2)}) collective-permute-start(f32[2,512]{1,0:T(2,128)S(1)} %get-tuple-element.23), channel_id=1, source_target_pairs={{16,0},{32,16},{48,32},{64,48},{80,64},{96,80},{112,96},{128,112},... | collective-permute-start | bytes 12296 | tf_op jit(solution)/shard_map/ppermute | solution.py:26
  569.2 23.1 %collective-permute-start.52 = (f32[2,512]{1,0:T(2,128)S(1)}, f32[2,512]{1,0:T(2,128)S(1)}, u32[]{:S(2)}, u32[]{:S(2)}) collective-permute-start(f32[2,512]{1,0:T(2,128)S(1)} %get-tuple-element.22), channel_id=1, source_target_pairs={{0,16},{16,32},{32,48},{48,64},{64,80},{80,96},{96,112},{112,128},... | collective-permute-start | bytes 12296 | tf_op jit(solution)/shard_map/ppermute | solution.py:25
  575.1 9.1 %collective-permute-start.47 = (f32[36,2]{1,0:T(8,128)S(1)}, f32[36,2]{1,0:T(8,128)S(1)}, u32[]{:S(2)}, u32[]{:S(2)}) collective-permute-start(f32[36,2]{1,0:T(8,128)S(1)} %get-tuple-element.51), channel_id=1, source_target_pairs={{1,0},{2,1},{3,2},{4,3},{5,4},{6,5},{7,6},{8,7},{9,8},{10,9},{11,1... | collective-permute-start | bytes 872 | tf_op jit(solution)/shard_map/ppermute | solution.py:26
  577.0 12.4 %collective-permute-start.46 = (f32[36,2]{1,0:T(8,128)S(1)}, f32[36,2]{1,0:T(8,128)S(1)}, u32[]{:S(2)}, u32[]{:S(2)}) collective-permute-start(f32[36,2]{1,0:T(8,128)S(1)} %get-tuple-element.50), channel_id=1, source_target_pairs={{0,1},{1,2},{2,3},{3,4},{4,5},{5,6},{6,7},{7,8},{8,9},{9,10},{10,1... | collective-permute-start | bytes 872 | tf_op jit(solution)/shard_map/ppermute | solution.py:25
  582.3 7.5 %collective-permute-start.51 = (f32[68,2]{1,0:T(8,128)S(1)}, f32[68,2]{1,0:T(8,128)S(1)}, u32[]{:S(2)}, u32[]{:S(2)}) collective-permute-start(f32[68,2]{1,0:T(8,128)S(1)} %get-tuple-element.36), channel_id=1, source_target_pairs={{1,0},{2,1},{3,2},{4,3},{5,4},{6,5},{7,6},{8,7},{9,8},{10,9},{11,1... | collective-permute-start | bytes 1640 | tf_op jit(solution)/shard_map/ppermute | solution.py:26
  592.4 8.9 %collective-permute-start.55 = (f32[132,2]{1,0:T(8,128)S(1)}, f32[132,2]{1,0:T(8,128)S(1)}, u32[]{:S(2)}, u32[]{:S(2)}) collective-permute-start(f32[132,2]{1,0:T(8,128)S(1)} %get-tuple-element.17), channel_id=1, source_target_pairs={{1,0},{2,1},{3,2},{4,3},{5,4},{6,5},{7,6},{8,7},{9,8},{10,9},{11,1... | collective-permute-start | bytes 3176 | tf_op jit(solution)/shard_map/ppermute | solution.py:26
  594.3 7.1 %collective-permute-start.54 = (f32[132,2]{1,0:T(8,128)S(1)}, f32[132,2]{1,0:T(8,128)S(1)}, u32[]{:S(2)}, u32[]{:S(2)}) collective-permute-start(f32[132,2]{1,0:T(8,128)S(1)} %get-tuple-element.16), channel_id=1, source_target_pairs={{0,1},{1,2},{2,3},{3,4},{4,5},{5,6},{6,7},{7,8},{8,9},{9,10},{10,1... | collective-permute-start | bytes 3176 | tf_op jit(solution)/shard_map/ppermute | solution.py:25
  (14 other events, 253.3 us)
where the time goes:
time: 633 us; the launch traced here: 622 us
  blocking collectives  343 us (54%)
  starting transfers between devices  200 us (32%)
  matrix products  38.8 us (6%)
  between operations  18.2 us (3%)
  waiting for transfers between devices  11.5 us (2%)
  other arithmetic  9.16 us (1%)
    psum x2, blocking collectives, norm_sum(): return lax.psum(level_products(residual, residual), ('lat', 'lon'))  217 us
    ppermute x28, starting transfers between devices, with_halo(): before = lax.ppermute(last, axis, up)  139 us
    psum x1, blocking collectives, body(): curv_sum = lax.psum(curv_local, ('lat', 'lon'))  108 us
    ppermute x28, starting transfers between devices, with_halo(): after = lax.ppermute(first, axis, down)  50.2 us
    dot_general x40, matrix products, matmul(): jnp.dot(left, right, precision=highest, preferred_element_type=jnp.float32)  38.8 us
    all_to_all x1, blocking collectives, body(): lax.all_to_all(final_surface, 'lon', split_axis=0, concat_axis=1, tiled=T...  17.1 us
  transfers between devices with their start and end apart: 57, of which 6 were waited for; matrix products, arithmetic and copies ran while one was open for 4% of the time, Pallas kernels for 0%

commit v1 on v0

v1 whole, which is shorter than its diff:
```python
import functools
import math

import jax
import jax.numpy as jnp
import numpy as np
from jax import lax
from jax.experimental import pallas as pl
from jax.experimental.pallas import tpu as pltpu
from jax.sharding import PartitionSpec as P

LEVELS = 4
SPACINGS = (8, 4, 2, 1)
SCALES = (0.02, 0.03, 0.05, 0.08)
HALO = 64
MARGIN = 4
MESH = pl.DeviceIdType.MESH
F32 = jnp.float32
BF16 = jnp.bfloat16


def weight(cells, nodes, spacing):
    numerator = np.abs(2 * cells - 2 * spacing * nodes - (spacing - 1))
    d = numerator / (5.0 * spacing)
    value = np.maximum(1.0 - d, 0.0) ** 6 * (35.0 * d * d + 18.0 * d + 3.0) / 3.0
    return value / math.sqrt(spacing)


def halves(table):
    table = np.asarray(table, np.float32)
    high = table.astype(BF16)
    low = (table - high.astype(np.float32)).astype(BF16)
    return jnp.asarray(high), jnp.asarray(low)


def lanes_of(width, spacing):
    return -(-(width // spacing) // 128) * 128


def tables(rows, cols):
    width = cols + 2 * HALO
    row_parts, col_parts = [], []
    for s in SPACINGS[:3]:
        nodes = np.arange(rows // s + 2 * MARGIN) - MARGIN
        row_parts.append(weight(np.arange(rows)[None, :], nodes[:, None], s))
        nodes = np.arange(width // s) - HALO // s
        part = np.zeros((width, lanes_of(width, s)))
        part[:, : width // s] = weight(np.arange(width)[:, None] - HALO, nodes[None, :], s)
        col_parts.append(part)
    back = np.concatenate(row_parts, axis=0)
    spread = np.zeros((rows, -(-back.shape[0] // 16) * 16))
    spread[:, : back.shape[0]] = back.T
    return (*halves(back), *halves(spread), *halves(np.concatenate(col_parts, axis=1)))


def split(x):
    high = x.astype(BF16)
    return high, (x - high.astype(F32)).astype(BF16)


def dot(a, b):
    return jnp.dot(a, b, preferred_element_type=F32)


def dot_t(a, b):
    return lax.dot_general(a, b, (((1,), (1,)), ((), ())), preferred_element_type=F32)


def roll(x, shift, axis):
    return pltpu.roll(x, shift % x.shape[axis], axis)


TAPS = [float(np.float32(weight(np.int64(0), np.int64(o), 1))) for o in range(3)]


def five(x, axis):
    near = roll(x, 1, axis) + roll(x, -1, axis)
    far = roll(x, 2, axis) + roll(x, -2, axis)
    return TAPS[0] * x + TAPS[1] * near + TAPS[2] * far


def stencil(x):
    return 5.0 * x - (roll(x, 1, 0) + roll(x, -1, 0) + roll(x, 1, 1) + roll(x, -1, 1))


def total(x):
    return jnp.sum(jnp.sum(x, axis=0, keepdims=True), axis=1, keepdims=True)


def kernel(n_lat, n_lon, *refs):
    (
        obs_ref, gau_ref, back_h, back_l, spread_h, spread_l, cols_h_hbm, cols_l_hbm,
        r0_out, r1_out, r2_out, r3_out, q0_out, q1_out, q2_out, q3_out, first_out, second_out, mix_out,
        cols_h, cols_l, obs_pad, obs_tile, gau_pad, gau_left, gau_right, extended,
        up_send, down_send, from_up, from_down, swath_src, swath_dst, red_src, red_lon, red_lat,
        table_sem, obs_sem, gau_sem, strip_sem, swath_sem, lon_sem, lat_sem,
    ) = refs
    r_out = (r0_out, r1_out, r2_out, r3_out)
    q_out = (q0_out, q1_out, q2_out, q3_out)
    lat, lon = lax.axis_index("lat"), lax.axis_index("lon")
    rows, cols = gau_ref.shape
    width = cols + 2 * HALO
    swath = obs_ref.shape[0]
    lanes = [lanes_of(width, s) for s in SPACINGS]
    starts = [sum(lanes[:k]) for k in range(LEVELS)]
    heights = [rows // s + 2 * MARGIN for s in SPACINGS]
    tops = [sum(heights[:k]) for k in range(LEVELS)]

    def lon_peer(d):
        return lax.rem(lon + d, n_lon)

    def lat_peer(d):
        return lax.rem(lat + d, n_lat)

    load_h = pltpu.make_async_copy(cols_h_hbm, cols_h, table_sem.at[0])
    load_l = pltpu.make_async_copy(cols_l_hbm, cols_l, table_sem.at[1])
    load_h.start()
    load_l.start()

    barrier = pltpu.get_barrier_semaphore()

    def greet_lon(d, c):
        pl.semaphore_signal(barrier, inc=1, device_id={"lon": lon_peer(d)}, device_id_type=MESH)
        return c

    def greet_lat(d, c):
        pl.semaphore_signal(barrier, inc=1, device_id={"lat": lat_peer(d)}, device_id_type=MESH)
        return c

    lax.fori_loop(1, n_lat, greet_lat, 0)
    lax.fori_loop(1, n_lon, greet_lon, 0)

    obs_pad[:, :128] = jnp.zeros((swath, 128), F32)
    obs_pad[:, n_lon * cols :] = jnp.zeros((swath, 128), F32)
    obs_pad[:, HALO : HALO + n_lon * cols] = obs_ref[...]
    gau_pad[:, :128] = jnp.zeros((rows, 128), F32)
    gau_pad[:, cols:] = jnp.zeros((rows, 128), F32)
    gau_pad[:, HALO : HALO + cols] = gau_ref[...].astype(F32)
    extended[...] = jnp.zeros_like(extended)

    pl.semaphore_wait(barrier, n_lat - 1 + n_lon - 1)

    def scatter(d, c):
        peer = lon_peer(d)
        pltpu.make_async_remote_copy(
            src_ref=obs_pad.at[:, pl.ds(pl.multiple_of(peer * cols, 128), width)],
            dst_ref=obs_tile.at[pl.ds(pl.multiple_of(lon * swath, 8), swath), :],
            send_sem=obs_sem.at[0],
            recv_sem=obs_sem.at[1],
            device_id={"lon": peer},
            device_id_type=MESH,
        ).start()
        return c

    def beside(src, dst, which, d):
        return pltpu.make_async_remote_copy(
            src_ref=src,
            dst_ref=dst,
            send_sem=gau_sem.at[2 * which],
            recv_sem=gau_sem.at[2 * which + 1],
            device_id={"lon": lon_peer(d)},
            device_id_type=MESH,
        )

    to_right = beside(gau_pad.at[:, cols:], gau_left, 0, 1)
    to_left = beside(gau_pad.at[:, :128], gau_right, 1, n_lon - 1)
    lax.fori_loop(1, n_lon, scatter, 0)
    to_right.start()
    to_left.start()
    own = pl.ds(pl.multiple_of(lon * swath, 8), swath)
    obs_tile[own, :] = obs_pad[:, pl.ds(pl.multiple_of(lon * cols, 128), width)]

    load_h.wait()
    load_l.wait()
    to_right.wait()
    to_left.wait()
    gau_pad[:, :128] += gau_left[...] * jnp.where(lon > 0, 1.0, 0.0)
    gau_pad[:, cols:] += gau_right[...] * jnp.where(lon < n_lon - 1, 1.0, 0.0)
    all_obs = obs_tile.at[: (n_lon - 1) * swath]
    pltpu.make_async_copy(all_obs, all_obs, obs_sem.at[1]).wait()
    pltpu.make_async_copy(all_obs, all_obs, obs_sem.at[0]).wait()

    valid = []
    inside = []
    for k, s in enumerate(SPACINGS):
        row = lax.broadcasted_iota(jnp.int32, (heights[k], 1), 0) - MARGIN
        col = lax.broadcasted_iota(jnp.int32, (1, lanes[k]), 1) - HALO // s
        row_global, col_global = row + lat * (rows // s), col + lon * (cols // s)
        row_ok = jnp.where((row_global >= 0) & (row_global < n_lat * (rows // s)), 1.0, 0.0)
        col_ok = jnp.where((col_global >= 0) & (col_global < n_lon * (cols // s)), 1.0, 0.0)
        valid.append(row_ok * col_ok)
        row_own = jnp.where((row >= 0) & (row < rows // s), 1.0, 0.0)
        col_own = jnp.where((col >= 0) & (col < cols // s), 1.0, 0.0)
        inside.append((row_own, col_own))

    def columns(k):
        at = slice(starts[k], starts[k] + lanes[k])
        return cols_h[:, at], cols_l[:, at]

    def adjoint(misfit):
        high, low = split(misfit)
        part = dot(back_h[...], high) + dot(back_h[...], low) + dot(back_l[...], high)
        result = []
        for k in range(3):
            high, low = split(part[tops[k] : tops[k] + heights[k]])
            table_h, table_l = columns(k)
            result.append(dot(high, table_h) + dot(high, table_l) + dot(low, table_h))
        extended[MARGIN : MARGIN + rows, :] = five(misfit, 1)
        result.append(five(extended[...], 0))
        return result

    def forward(coeffs):
        parts = []
        for k in range(3):
            high, low = split(coeffs[k])
            table_h, table_l = columns(k)
            parts.append(dot_t(high, table_h) + dot_t(high, table_l) + dot_t(low, table_h))
        fill = spread_h.shape[1] - sum(heights[:3])
        if fill:
            parts.append(jnp.zeros((fill, width), F32))
        high, low = split(jnp.concatenate(parts, axis=0))
        coarse = dot(spread_h[...], high) + dot(spread_h[...], low) + dot(spread_l[...], high)
        fine = five(coeffs[3], 0)[MARGIN : MARGIN + rows]
        return coarse + five(fine, 1)

    def strips(which, partial):
        for k in range(LEVELS):
            at = slice(starts[k], starts[k] + lanes[k])
            up_send[which, :, at] = partial[k][:8]
            down_send[which, :, at] = partial[k][heights[k] - 8 :]
        copies = []
        for j, (src, dst, d) in enumerate(((up_send, from_down, n_lat - 1), (down_send, from_up, 1))):
            copies.append(
                pltpu.make_async_remote_copy(
                    src_ref=src.at[which],
                    dst_ref=dst.at[which],
                    send_sem=strip_sem.at[4 * which + 2 * j],
                    recv_sem=strip_sem.at[4 * which + 2 * j + 1],
                    device_id={"lat": lat_peer(d)},
                    device_id_type=MESH,
                )
            )
            copies[-1].start()
        return copies

    def joined(which, partial):
        result = []
        has_up = jnp.where(lat > 0, 1.0, 0.0)
        has_down = jnp.where(lat < n_lat - 1, 1.0, 0.0)
        for k in range(LEVELS):
            at = slice(starts[k], starts[k] + lanes[k])
            head = partial[k][:8] + has_up * from_up[which, :, at]
            tail = partial[k][heights[k] - 8 :] + has_down * from_down[which, :, at]
            middle = partial[k][8 : heights[k] - 8]
            result.append(jnp.concatenate([head, middle, tail], axis=0) * valid[k])
        return result

    def send_swaths(which, surface):
        swath_src[which] = surface[:, HALO : HALO + cols]

        def push(d, c):
            peer = lon_peer(d)
            pltpu.make_async_remote_copy(
                src_ref=swath_src.at[which, pl.ds(pl.multiple_of(peer * swath, 8), swath), :],
                dst_ref=swath_dst.at[which, :, pl.ds(pl.multiple_of(lon * cols, 128), cols)],
                send_sem=swath_sem.at[2 * which],
                recv_sem=swath_sem.at[2 * which + 1],
                device_id={"lon": peer},
                device_id_type=MESH,
            ).start()
            return c

        lax.fori_loop(1, n_lon, push, 0)
        at = pl.ds(pl.multiple_of(lon * cols, 128), cols)
        swath_dst[which, :, at] = swath_src[which, own, :]

    def extract(k, x):
        s = SPACINGS[k]
        return x[MARGIN : MARGIN + rows // s, HALO // s : HALO // s + cols // s]

    def squares(k, x):
        row_own, col_own = inside[k]
        return total(x * x * row_own * col_own)

    lane = lax.broadcasted_iota(jnp.int32, (1, width), 1)
    own_lane = jnp.where((lane >= HALO) & (lane < HALO + cols), 1.0, 0.0)
    gauge = gau_pad[...]

    partial = adjoint(2.0 * gauge * obs_tile[...])
    copies = strips(0, partial)
    for copy in copies:
        copy.wait()
    right = joined(0, partial)

    surface = forward(right)
    misfit = 2.0 * gauge * surface
    partial = adjoint(misfit)
    copies = strips(1, partial)
    send_swaths(0, surface)
    mu0 = jnp.zeros((1, 1), F32)
    mu1 = total(misfit * surface * own_lane)
    rough = []
    for k in range(LEVELS):
        smooth = stencil(right[k]) * valid[k]
        rough.append(SCALES[k] * stencil(smooth) * valid[k])
        mu0 = mu0 + squares(k, right[k])
        mu1 = mu1 + SCALES[k] * squares(k, smooth)
        r_out[k][...] = extract(k, right[k])
    for copy in copies:
        copy.wait()
    image = [x + y for x, y in zip(joined(1, partial), rough)]

    surface = forward(image)
    mu2 = jnp.zeros((1, 1), F32)
    mu3 = total(2.0 * gauge * surface * surface * own_lane)
    for k in range(LEVELS):
        mu2 = mu2 + squares(k, image[k])
        mu3 = mu3 + SCALES[k] * squares(k, stencil(image[k]) * valid[k])

    def placed(values):
        at = lax.broadcasted_iota(jnp.int32, (1, 128), 1)
        row = jnp.zeros((1, 128), F32)
        for i, value in enumerate(values):
            row = row + jnp.where(at == i, value, 0.0)
        return row

    def reduce_start(stage, value, dst, sem, count, axis, peer_of):
        red_src[stage] = value

        def push(d, c):
            pltpu.make_async_remote_copy(
                src_ref=red_src.at[stage],
                dst_ref=dst.at[d - 1],
                send_sem=sem.at[0],
                recv_sem=sem.at[1],
                device_id={axis: peer_of(d)},
                device_id_type=MESH,
            ).start()
            return c

        lax.fori_loop(1, count, push, 0)

    def reduce_end(value, dst, sem):
        pltpu.make_async_copy(dst, dst, sem.at[1]).wait()
        pltpu.make_async_copy(dst, dst, sem.at[0]).wait()
        return value + jnp.sum(dst[...], axis=0)

    moments = placed((mu0, mu1, mu2, mu3))
    reduce_start(0, moments, red_lon, lon_sem, n_lon, "lon", lon_peer)
    send_swaths(1, surface)
    for k in range(LEVELS):
        q_out[k][...] = extract(k, image[k])
    moments = reduce_end(moments, red_lon, lon_sem)
    reduce_start(1, moments, red_lat, lat_sem, n_lat, "lat", lat_peer)
    moments = reduce_end(moments, red_lat, lat_sem)

    m0, m1, m2, m3 = (moments[:, i : i + 1] for i in range(4))
    alpha = m0 / m1
    grow = alpha * m2 / m1
    second_norm = alpha * alpha * m2 - m0
    curv = alpha * alpha * m3 - grow * grow * m1
    gamma = second_norm / curv
    mix_out[...] = placed((alpha + gamma * grow, -alpha * gamma))

    everything = swath_dst.at[0, :, : (n_lon - 1) * cols]
    for i in range(4):
        pltpu.make_async_copy(everything, everything, swath_sem.at[i]).wait()
    first_out[...] = swath_dst[0]
    second_out[...] = swath_dst[1]


def combine(*refs):
    mix = refs[0][...]
    a, b = mix[:, 0:1], mix[:, 1:2]
    count = LEVELS + 1
    for first, second, out in zip(refs[1 : 1 + count], refs[1 + count : 1 + 2 * count], refs[1 + 2 * count :]):
        out[...] = a * first[...] + b * second[...]


def body(observed, gauged):
    n_lat, n_lon = lax.axis_size("lat"), lax.axis_size("lon")
    rows, cols = gauged.shape
    swath = observed.shape[0]
    width = cols + 2 * HALO
    back_h, back_l, spread_h, spread_l, cols_h, cols_l = tables(rows, cols)
    level_shapes = [jax.ShapeDtypeStruct((rows // s, cols // s), F32) for s in SPACINGS]
    swath_shape = jax.ShapeDtypeStruct(observed.shape, F32)
    strip = 8 * sum(lanes_of(width, s) for s in SPACINGS)
    vmem = pl.BlockSpec(memory_space=pltpu.VMEM)
    anywhere = pl.BlockSpec(memory_space=pl.ANY)
    dma = pltpu.SemaphoreType.DMA
    *pieces, mix = pl.pallas_call(
        functools.partial(kernel, n_lat, n_lon),
        out_shape=(
            *level_shapes,
            *level_shapes,
            swath_shape,
            swath_shape,
            jax.ShapeDtypeStruct((1, 128), F32),
        ),
        in_specs=[vmem] * 6 + [anywhere] * 2,
        out_specs=[vmem] * 11,
        scratch_shapes=[
            pltpu.VMEM(cols_h.shape, BF16),
            pltpu.VMEM(cols_l.shape, BF16),
            pltpu.VMEM((swath, n_lon * cols + 2 * HALO), F32),
            pltpu.VMEM((rows, width), F32),
            pltpu.VMEM((rows, width), F32),
            pltpu.VMEM((rows, 128), F32),
            pltpu.VMEM((rows, 128), F32),
            pltpu.VMEM((rows + 2 * MARGIN, width), F32),
            *[pltpu.VMEM((2, 8, strip // 8), F32)] * 4,
            pltpu.VMEM((2, rows, cols), F32),
            pltpu.VMEM((2, swath, n_lon * cols), F32),
            pltpu.VMEM((2, 1, 128), F32),
            pltpu.VMEM((n_lon - 1, 1, 128), F32),
            pltpu.VMEM((n_lat - 1, 1, 128), F32),
            dma((2,)),
            dma((2,)),
            dma((4,)),
            dma((8,)),
            dma((4,)),
            dma((2,)),
            dma((2,)),
        ],
        compiler_params=pltpu.CompilerParams(collective_id=0, has_side_effects=True),
        name="krylov",
    )(observed, gauged, back_h, back_l, spread_h, spread_l, cols_h, cols_l)
    firsts = [*pieces[:LEVELS], pieces[2 * LEVELS]]
    seconds = [*pieces[LEVELS : 2 * LEVELS], pieces[2 * LEVELS + 1]]
    return pl.pallas_call(
        combine,
        out_shape=(*level_shapes, swath_shape),
        in_specs=[vmem] * 11,
        out_specs=[vmem] * 5,
        name="combine",
    )(mix, *firsts, *seconds)


def solution(mesh):
    tile = P("lat", "lon")
    swaths = P(("lat", "lon"), None)
    return jax.shard_map(
        body,
        mesh=mesh,
        in_specs=(swaths, tile),
        out_specs=(tile, tile, tile, tile, swaths),
        check_vma=False,
    )
```

time: 633 us -> 55.1 us (0.09); the launches traced: 622 us -> 54.9 us
  blocking collectives: 343 us -> 0 us
  starting transfers between devices: 200 us -> 0 us
  Pallas kernels: 0 us -> 54.2 us
  matrix products: 38.8 us -> 0 us
  between operations: 18.2 us -> 0.64 us
  waiting for transfers between devices: 11.5 us -> 0 us
  other arithmetic: 9.16 us -> 0 us
    psum x3 -> x0, blocking collectives: 326 us -> none  [the longest x2 217 us: norm_sum(): return lax.psum(level_products(residual, residual), ('lat', 'lon'))]
    ppermute x56 -> x0, starting transfers between devices: 189 us -> none  [the longest x28 139 us: with_halo(): before = lax.ppermute(last, axis, up)]
    pallas_call x0 -> x2, Pallas kernels: none -> 54.2 us  [the longest x1 52 us: body(): pl.pallas_call(functools.partial(kernel, n_lat, n_lon), out_shape=(*level...]
    dot_general x40 -> x0, matrix products: 38.8 us -> none  [matmul(): jnp.dot(left, right, precision=highest, preferred_element_type=jnp.float32)]
    all_to_all x1 -> x0, blocking collectives: 17.1 us -> none  [body(): lax.all_to_all(final_surface, 'lon', split_axis=0, concat_axis=1, tiled=T...]
    all_to_all x1 -> x0, starting transfers between devices: 10.3 us -> none  [body(): lax.all_to_all(observed, 'lon', split_axis=1, concat_axis=0, tiled=True)]
    all_to_all x1 -> x0, waiting for transfers between devices: 8.25 us -> none  [body(): lax.all_to_all(observed, 'lon', split_axis=1, concat_axis=0, tiled=True)]
  transfers between devices with their start and end apart: 57 -> 0, of which waited for: 6 -> 0; matrix products, arithmetic and copies ran while one was open for 4% -> 0% of each run, Pallas kernels for 0% -> 0%
where the time goes in v1:
time: 55.1 us; the launch traced here: 54.9 us
  Pallas kernels  54.2 us (98%)
  between operations  0.64 us (1%)
    pallas_call x1, Pallas kernels, body(): pl.pallas_call(functools.partial(kernel, n_lat, n_lon), out_shape=(*level...  52 us
    pallas_call x1, Pallas kernels, body(): pl.pallas_call(combine, out_shape=(*level_shapes, swath_shape), in_specs=...  2.24 us

profile of v1, /device:TPU:1, one launch (start us, length us, event | category | flops | bytes accessed | tf_op | source)
XLA Modules:
  0.0 54.9 jit_solution(13697480242652233150)
XLA Ops:
  0.6 52.0 %krylov.1 = (f32[16,64]{1,0:T(8,128)}, f32[32,128]{1,0:T(8,128)}, f32[64,256]{1,0:T(8,128)}, f32[128,512]{1,0:T(8,128)}, f32[16,64]{1,0:T(8,128)}, /*index=5*/f3...) custom-call(f32[8,8192]{1,0:T(8,128)} %refs_0_.1, ...), custom_call_target="tpu_custom_call" | custom-call | tf_op jit(solution)/shard_map/krylov/pallas_call | solution.py:392
  52.6 2.2 %combine.1 = (f32[16,64]{1,0:T(8,128)}, f32[32,128]{1,0:T(8,128)}, f32[64,256]{1,0:T(8,128)}, f32[128,512]{1,0:T(8,128)}, f32[8,8192]{1,0:T(8,128)}) custom-call(f32[1,128]{1,0:T(1,128)} %get-tuple-element.16.refs_0_, f32[16,64]{1,0:T(8,128)} %get-tuple-element.17.refs_1_, f32[32,128]{1,0:T(8,128)} %get-tuple-element.18.refs_2_, ...), custom_call_target="tpu_custom_call" | custom-call | tf_op jit(solution)/shard_map/combine/pallas_call | solution.py:431

commit v2 on v1

v2 whole, which is shorter than its diff:
```python
import functools
import math

import jax
import jax.numpy as jnp
import numpy as np
from jax import lax
from jax.experimental import pallas as pl
from jax.experimental.pallas import tpu as pltpu
from jax.sharding import PartitionSpec as P

LEVELS = 4
SPACINGS = (8, 4, 2, 1)
SCALES = (0.02, 0.03, 0.05, 0.08)
HALO = 64
MARGIN = 4
MESH = pl.DeviceIdType.MESH
F32 = jnp.float32
BF16 = jnp.bfloat16


def weight(cells, nodes, spacing):
    numerator = np.abs(2 * cells - 2 * spacing * nodes - (spacing - 1))
    d = numerator / (5.0 * spacing)
    value = np.maximum(1.0 - d, 0.0) ** 6 * (35.0 * d * d + 18.0 * d + 3.0) / 3.0
    return value / math.sqrt(spacing)


def halves(table):
    table = np.asarray(table, np.float32)
    high = table.astype(BF16)
    low = (table - high.astype(np.float32)).astype(BF16)
    return jnp.asarray(np.concatenate([high, low], axis=0))


def lanes_of(width, spacing):
    return -(-(width // spacing) // 128) * 128


def tables(rows, cols):
    width = cols + 2 * HALO
    row_parts, col_parts = [], []
    for s in SPACINGS[:3]:
        nodes = np.arange(rows // s + 2 * MARGIN) - MARGIN
        row_parts.append(weight(np.arange(rows)[None, :], nodes[:, None], s))
        nodes = np.arange(width // s) - HALO // s
        part = np.zeros((width, lanes_of(width, s)))
        part[:, : width // s] = weight(np.arange(width)[:, None] - HALO, nodes[None, :], s)
        col_parts.append(part)
    back = np.concatenate(row_parts, axis=0)
    spread = np.zeros((rows, 128 * len(row_parts)))
    for k, part in enumerate(row_parts):
        spread[:, 128 * k : 128 * k + part.shape[0]] = part.T
    return halves(back), halves(spread), halves(np.concatenate(col_parts, axis=1))


def halve(x):
    high = x.astype(BF16).astype(F32)
    return jnp.concatenate([high, x - high], axis=0).astype(BF16)


def times(x, high, low, transposed=False):
    contract = (((1,), (1 if transposed else 0,)), ((), ()))
    n = x.shape[0]
    x = halve(x)
    both = lax.dot_general(x, high, contract, preferred_element_type=F32)
    rest = lax.dot_general(x[:n], low, contract, preferred_element_type=F32)
    return both[:n] + both[n:] + rest


def into(table, x):
    n = table.shape[0] // 2
    high = x.astype(BF16)
    low = (x - high.astype(F32)).astype(BF16)
    both = jnp.dot(table, high, preferred_element_type=F32)
    rest = jnp.dot(table[:n], low, preferred_element_type=F32)
    return both[:n] + both[n:] + rest


def roll(x, shift, axis):
    return pltpu.roll(x, shift % x.shape[axis], axis)


TAPS = [float(np.float32(weight(np.int64(0), np.int64(o), 1))) for o in range(3)]


def five(x, axis):
    near = roll(x, 1, axis) + roll(x, -1, axis)
    far = roll(x, 2, axis) + roll(x, -2, axis)
    return TAPS[0] * x + TAPS[1] * near + TAPS[2] * far


def stencil(x):
    return 5.0 * x - (roll(x, 1, 0) + roll(x, -1, 0) + roll(x, 1, 1) + roll(x, -1, 1))


def fold(x):
    return jnp.sum(x.reshape(x.shape[0] // 8, 8, x.shape[1]), axis=0)


def fold_lanes(x):
    result = x[:, :128]
    for at in range(128, x.shape[1], 128):
        result = result + x[:, at : at + 128]
    return result


def kernel(n_lat, n_lon, *refs):
    (
        obs_hbm, gau_hbm, back_hbm, spread_hbm, cols_hbm,
        r0_out, r1_out, r2_out, r3_out, q0_out, q1_out, q2_out, q3_out, first_out, second_out, mix_out,
        obs_ref, gau_ref, back, spread, table, obs_pad, obs_tile, gau_pad, gau_send, gau_recv, extended,
        up_send, down_send, from_up, from_down, swath_src, swath_dst, red_src, red_plane, red_line,
        load_sem, obs_sem, gau_sem, strip_sem, swath_sem, plane_sem, line_sem,
    ) = refs
    r_out = (r0_out, r1_out, r2_out, r3_out)
    q_out = (q0_out, q1_out, q2_out, q3_out)
    lat, lon = lax.axis_index("lat"), lax.axis_index("lon")
    rows, cols = gau_hbm.shape
    width = cols + 2 * HALO
    swath = obs_hbm.shape[0]
    lanes = [lanes_of(width, s) for s in SPACINGS]
    starts = [sum(lanes[:k]) for k in range(LEVELS)]
    heights = [rows // s + 2 * MARGIN for s in SPACINGS]
    tops = [sum(heights[:k]) for k in range(LEVELS)]

    def lon_peer(d):
        return lax.rem(lon + d, n_lon)

    def lat_peer(d):
        return lax.rem(lat + d, n_lat)

    def plane_peer(e):
        twin = lat + 1 - 2 * lax.rem(lat, 2)
        return {"lat": jnp.where(e >= n_lon, twin, lat), "lon": lon_peer(e)}

    def line_peer(f):
        return {"lat": lat_peer(2 * f)}

    barrier = pltpu.get_barrier_semaphore()

    def greet_line(f, c):
        pl.semaphore_signal(barrier, inc=1, device_id=line_peer(f), device_id_type=MESH)
        return c

    def greet_plane(e, c):
        pl.semaphore_signal(barrier, inc=1, device_id=plane_peer(e), device_id_type=MESH)
        return c

    beyond = {"lat": lax.rem(lat + n_lat - 1 + 2 * lax.rem(lat, 2), n_lat)}
    lax.fori_loop(1, n_lat // 2, greet_line, 0)
    pl.semaphore_signal(barrier, inc=1, device_id=beyond, device_id_type=MESH)
    lax.fori_loop(1, 2 * n_lon, greet_plane, 0)

    loads = [
        pltpu.make_async_copy(src, dst, load_sem.at[i])
        for i, (src, dst) in enumerate(
            ((obs_hbm, obs_ref), (gau_hbm, gau_ref), (back_hbm, back), (spread_hbm, spread), (cols_hbm, table))
        )
    ]
    for load in loads:
        load.start()
    extended[...] = jnp.zeros_like(extended)
    for load in loads:
        load.wait()
    obs_pad[:, :128] = jnp.zeros((swath, 128), F32)
    obs_pad[:, n_lon * cols :] = jnp.zeros((swath, 128), F32)
    obs_pad[:, HALO : HALO + n_lon * cols] = obs_ref[...]
    gau_pad[:, :128] = jnp.zeros((rows, 128), F32)
    gau_pad[:, cols:] = jnp.zeros((rows, 128), F32)
    gauge = gau_ref[...].astype(F32)
    gau_pad[:, HALO : HALO + cols] = gauge
    half = rows // 2
    lane = lax.broadcasted_iota(jnp.int32, (half, 128), 1)
    last, first = gauge[:, cols - 128 :], gauge[:, :128]
    gau_send[0] = jnp.where(lane < HALO, roll(last[:half], HALO, 1), last[half:])
    gau_send[1] = jnp.where(lane < HALO, first[:half], roll(first[half:], HALO, 1))

    pl.semaphore_wait(barrier, n_lat // 2 - 1 + 1 + 2 * n_lon - 1)

    def scatter(d, c):
        peer = lon_peer(d)
        pltpu.make_async_remote_copy(
            src_ref=obs_pad.at[:, pl.ds(pl.multiple_of(peer * cols, 128), width)],
            dst_ref=obs_tile.at[pl.ds(pl.multiple_of(lon * swath, 8), swath), :],
            send_sem=obs_sem.at[0],
            recv_sem=obs_sem.at[1],
            device_id={"lon": peer},
            device_id_type=MESH,
        ).start()
        return c

    def beside(which, d):
        return pltpu.make_async_remote_copy(
            src_ref=gau_send.at[which],
            dst_ref=gau_recv.at[which],
            send_sem=gau_sem.at[2 * which],
            recv_sem=gau_sem.at[2 * which + 1],
            device_id={"lon": lon_peer(d)},
            device_id_type=MESH,
        )

    to_right, to_left = beside(0, 1), beside(1, n_lon - 1)
    lax.fori_loop(1, n_lon, scatter, 0)
    to_right.start()
    to_left.start()
    own = pl.ds(pl.multiple_of(lon * swath, 8), swath)
    obs_tile[own, :] = obs_pad[:, pl.ds(pl.multiple_of(lon * cols, 128), width)]

    to_right.wait()
    to_left.wait()
    packed = gau_recv[0] * jnp.where(lon > 0, 1.0, 0.0)
    gau_pad[:half, :128] = jnp.where(lane < HALO, packed, gau_pad[:half, :128])
    gau_pad[half:, :128] = jnp.where(lane < HALO, roll(packed, HALO, 1), gau_pad[half:, :128])
    packed = gau_recv[1] * jnp.where(lon < n_lon - 1, 1.0, 0.0)
    gau_pad[:half, cols:] = jnp.where(lane < HALO, gau_pad[:half, cols:], roll(packed, HALO, 1))
    gau_pad[half:, cols:] = jnp.where(lane < HALO, gau_pad[half:, cols:], packed)
    all_obs = obs_tile.at[: (n_lon - 1) * swath]
    pltpu.make_async_copy(all_obs, all_obs, obs_sem.at[1]).wait()
    pltpu.make_async_copy(all_obs, all_obs, obs_sem.at[0]).wait()

    valid = []
    inside = []
    for k, s in enumerate(SPACINGS):
        row = lax.broadcasted_iota(jnp.int32, (heights[k], 1), 0) - MARGIN
        col = lax.broadcasted_iota(jnp.int32, (1, lanes[k]), 1) - HALO // s
        row_global, col_global = row + lat * (rows // s), col + lon * (cols // s)
        row_ok = jnp.where((row_global >= 0) & (row_global < n_lat * (rows // s)), 1.0, 0.0)
        col_ok = jnp.where((col_global >= 0) & (col_global < n_lon * (cols // s)), 1.0, 0.0)
        valid.append(row_ok * col_ok)
        inside.append(jnp.where((col >= 0) & (col < cols // s), 1.0, 0.0))

    def adjoint(misfit):
        part = into(back[...], misfit)
        result = []
        for k in range(3):
            at = slice(starts[k], starts[k] + lanes[k])
            result.append(times(part[tops[k] : tops[k] + heights[k]], table[:width, at], table[width:, at]))
        extended[MARGIN : MARGIN + rows, :] = five(misfit, 1)
        result.append(five(extended[...], 0))
        return result

    def forward(coeffs):
        parts = [into(spread[:, 128 * k : 128 * k + heights[k]], coeffs[k]) for k in range(3)]
        coarse = times(jnp.concatenate(parts, axis=1), table[:width], table[width:], transposed=True)
        fine = five(coeffs[3], 0)[MARGIN : MARGIN + rows]
        return coarse + five(fine, 1)

    def strips(which, partial):
        for k in range(LEVELS):
            at = slice(starts[k], starts[k] + lanes[k])
            up_send[which, :, at] = partial[k][:8]
            down_send[which, :, at] = partial[k][heights[k] - 8 :]
        copies = []
        for j, (src, dst, d) in enumerate(((up_send, from_down, n_lat - 1), (down_send, from_up, 1))):
            copies.append(
                pltpu.make_async_remote_copy(
                    src_ref=src.at[which],
                    dst_ref=dst.at[which],
                    send_sem=strip_sem.at[4 * which + 2 * j],
                    recv_sem=strip_sem.at[4 * which + 2 * j + 1],
                    device_id={"lat": lat_peer(d)},
                    device_id_type=MESH,
                )
            )
            copies[-1].start()
        return copies

    def joined(which, partial):
        result = []
        has_up = jnp.where(lat > 0, 1.0, 0.0)
        has_down = jnp.where(lat < n_lat - 1, 1.0, 0.0)
        for k in range(LEVELS):
            at = slice(starts[k], starts[k] + lanes[k])
            head = partial[k][:8] + has_up * from_up[which, :, at]
            tail = partial[k][heights[k] - 8 :] + has_down * from_down[which, :, at]
            middle = partial[k][8 : heights[k] - 8]
            result.append(jnp.concatenate([head, middle, tail], axis=0) * valid[k])
        return result

    def send_swaths(which):
        def push(d, c):
            peer = lon_peer(d)
            pltpu.make_async_remote_copy(
                src_ref=swath_src.at[which, pl.ds(pl.multiple_of(peer * swath, 8), swath), :],
                dst_ref=swath_dst.at[which, :, pl.ds(pl.multiple_of(lon * cols, 128), cols)],
                send_sem=swath_sem.at[2 * which],
                recv_sem=swath_sem.at[2 * which + 1],
                device_id={"lon": peer},
                device_id_type=MESH,
            ).start()
            return c

        lax.fori_loop(1, n_lon, push, 0)
        at = pl.ds(pl.multiple_of(lon * cols, 128), cols)
        swath_dst[which, :, at] = swath_src[which, own, :]

    def extract(k, x):
        s = SPACINGS[k]
        return x[MARGIN : MARGIN + rows // s, HALO // s : HALO // s + cols // s]

    above = lax.broadcasted_iota(jnp.int32, (8, 1), 0) >= MARGIN

    def squares(k, x):
        y = x * x
        n = heights[k]
        ends = jnp.where(above, y[:8], 0.0) + jnp.where(above, 0.0, y[n - 8 :])
        return fold_lanes((fold(y[8 : n - 8]) + ends) * inside[k])

    lane = lax.broadcasted_iota(jnp.int32, (1, width), 1)
    own_lane = jnp.where((lane >= HALO) & (lane < HALO + cols), 1.0, 0.0)

    def misfits(surface):
        misfit = 2.0 * gau_pad[...] * surface
        return misfit, fold_lanes(fold(misfit * surface) * own_lane)

    partial = adjoint(2.0 * gau_pad[...] * obs_tile[...])
    copies = strips(0, partial)
    for copy in copies:
        copy.wait()
    right = joined(0, partial)

    surface = forward(right)
    misfit, mu1 = misfits(surface)
    partial = adjoint(misfit)
    copies = strips(1, partial)
    swath_src[0] = surface[:, HALO : HALO + cols]
    send_swaths(0)
    mu0 = jnp.zeros((8, 128), F32)
    rough = []
    for k in range(LEVELS):
        smooth = stencil(right[k]) * valid[k]
        rough.append(SCALES[k] * stencil(smooth) * valid[k])
        mu0 = mu0 + squares(k, right[k])
        mu1 = mu1 + SCALES[k] * squares(k, smooth)
        r_out[k][...] = extract(k, right[k])
    for copy in copies:
        copy.wait()
    image = [x + y for x, y in zip(joined(1, partial), rough)]

    surface = forward(image)
    mu2 = jnp.zeros((8, 128), F32)
    _, mu3 = misfits(surface)
    for k in range(LEVELS):
        mu2 = mu2 + squares(k, image[k])
        mu3 = mu3 + SCALES[k] * squares(k, stencil(image[k]) * valid[k])

    row8 = lax.broadcasted_iota(jnp.int32, (8, 128), 0)
    lane8 = lax.broadcasted_iota(jnp.int32, (8, 128), 1)

    def reduce_start(stage, value, dst, sem, count, peer_of):
        red_src[stage] = value

        def push(d, c):
            pltpu.make_async_remote_copy(
                src_ref=red_src.at[stage],
                dst_ref=dst.at[d - 1],
                send_sem=sem.at[0],
                recv_sem=sem.at[1],
                device_id=peer_of(d),
                device_id_type=MESH,
            ).start()
            return c

        lax.fori_loop(1, count, push, 0)

    def reduce_end(value, dst, sem):
        pltpu.make_async_copy(dst, dst, sem.at[1]).wait()
        return value + jnp.sum(dst[...], axis=0)

    gathered = jnp.zeros((8, 128), F32)
    for i, value in enumerate((mu0, mu1, mu2, mu3)):
        gathered = gathered + jnp.where(row8 == i, jnp.sum(value, axis=0, keepdims=True), 0.0)
    gathered = jnp.sum(gathered, axis=1, keepdims=True)
    moments = jnp.sum(jnp.where(row8 == lane8, gathered, 0.0), axis=0, keepdims=True)
    reduce_start(0, moments, red_plane, plane_sem, 2 * n_lon, plane_peer)
    swath_src[1] = surface[:, HALO : HALO + cols]
    for k in range(LEVELS):
        q_out[k][...] = extract(k, image[k])
    moments = reduce_end(moments, red_plane, plane_sem)
    reduce_start(1, moments, red_line, line_sem, n_lat // 2, line_peer)
    send_swaths(1)
    moments = reduce_end(moments, red_line, line_sem)

    m0, m1, m2, m3 = (moments[:, i : i + 1] for i in range(4))
    alpha = m0 / m1
    grow = alpha * m2 / m1
    second_norm = alpha * alpha * m2 - m0
    curv = alpha * alpha * m3 - grow * grow * m1
    gamma = second_norm / curv
    lane1 = lane8[:1]
    mix_out[...] = jnp.where(lane1 == 0, alpha + gamma * grow, 0.0) + jnp.where(lane1 == 1, -alpha * gamma, 0.0)

    everything = swath_dst.at[0, :, : (n_lon - 1) * cols]
    for i in range(4):
        pltpu.make_async_copy(everything, everything, swath_sem.at[i]).wait()
    pltpu.make_async_copy(red_plane, red_plane, plane_sem.at[0]).wait()
    pltpu.make_async_copy(red_line, red_line, line_sem.at[0]).wait()
    first_out[...] = swath_dst[0]
    second_out[...] = swath_dst[1]


def combine(*refs):
    mix = refs[0][...]
    a, b = mix[:, 0:1], mix[:, 1:2]
    count = LEVELS + 1
    for first, second, out in zip(refs[1 : 1 + count], refs[1 + count : 1 + 2 * count], refs[1 + 2 * count :]):
        out[...] = a * first[...] + b * second[...]


def body(observed, gauged):
    n_lat, n_lon = lax.axis_size("lat"), lax.axis_size("lon")
    rows, cols = gauged.shape
    swath = observed.shape[0]
    width = cols + 2 * HALO
    back, spread, table = tables(rows, cols)
    level_shapes = [jax.ShapeDtypeStruct((rows // s, cols // s), F32) for s in SPACINGS]
    swath_shape = jax.ShapeDtypeStruct(observed.shape, F32)
    strip = 8 * sum(lanes_of(width, s) for s in SPACINGS)
    vmem = pl.BlockSpec(memory_space=pltpu.VMEM)
    anywhere = pl.BlockSpec(memory_space=pl.ANY)
    dma = pltpu.SemaphoreType.DMA
    *pieces, mix = pl.pallas_call(
        functools.partial(kernel, n_lat, n_lon),
        out_shape=[pltpu.VMEM(x.shape, F32) for x in (*level_shapes, *level_shapes, swath_shape, swath_shape)]
        + [pltpu.VMEM((1, 128), F32)],
        in_specs=[anywhere] * 5,
        out_specs=[vmem] * 11,
        scratch_shapes=[
            pltpu.VMEM(observed.shape, F32),
            pltpu.VMEM(gauged.shape, gauged.dtype),
            pltpu.VMEM(back.shape, BF16),
            pltpu.VMEM(spread.shape, BF16),
            pltpu.VMEM(table.shape, BF16),
            pltpu.VMEM((swath, n_lon * cols + 2 * HALO), F32),
            pltpu.VMEM((rows, width), F32),
            pltpu.VMEM((rows, width), F32),
            pltpu.VMEM((2, rows // 2, 128), F32),
            pltpu.VMEM((2, rows // 2, 128), F32),
            pltpu.VMEM((rows + 2 * MARGIN, width), F32),
            *[pltpu.VMEM((2, 8, strip // 8), F32)] * 4,
            pltpu.VMEM((2, rows, cols), F32),
            pltpu.VMEM((2, swath, n_lon * cols), F32),
            pltpu.VMEM((2, 1, 128), F32),
            pltpu.VMEM((2 * n_lon - 1, 1, 128), F32),
            pltpu.VMEM((n_lat // 2 - 1, 1, 128), F32),
            dma((5,)),
            dma((2,)),
            dma((4,)),
            dma((8,)),
            dma((4,)),
            dma((2,)),
            dma((2,)),
        ],
        compiler_params=pltpu.CompilerParams(collective_id=0, has_side_effects=True),
        name="krylov",
    )(observed, gauged, back, spread, table)
    mix, *pieces = [pltpu.with_memory_space_constraint(x, pltpu.VMEM) for x in (mix, *pieces)]
    firsts = [*pieces[:LEVELS], pieces[2 * LEVELS]]
    seconds = [*pieces[LEVELS : 2 * LEVELS], pieces[2 * LEVELS + 1]]
    return pl.pallas_call(
        combine,
        out_shape=(*level_shapes, swath_shape),
        in_specs=[vmem] * 11,
        out_specs=[vmem] * 5,
        name="combine",
    )(mix, *firsts, *seconds)


def solution(mesh):
    tile = P("lat", "lon")
    swaths = P(("lat", "lon"), None)
    return jax.shard_map(
        body,
        mesh=mesh,
        in_specs=(swaths, tile),
        out_specs=(tile, tile, tile, tile, swaths),
        check_vma=False,
    )
```

time: 55.1 us -> 49.8 us (0.904)
  Pallas kernels: 54.2 us -> 49 us
    pallas_call x1, Pallas kernels: 52 us -> 48.1 us  [body(): pl.pallas_call(functools.partial(kernel, n_lat, n_lon), out_shape=[pltpu....]
    pallas_call x1, Pallas kernels: 2.24 us -> 0.94 us  [body(): pl.pallas_call(combine, out_shape=(*level_shapes, swath_shape), in_specs=...]
where the time goes in v2:
time: 49.8 us; the launch traced here: 49.7 us
  Pallas kernels  49 us (98%)
  between operations  0.64 us (1%)
    pallas_call x1, Pallas kernels, body(): pl.pallas_call(functools.partial(kernel, n_lat, n_lon), out_shape=[pltpu....  48.1 us

profile of v2, /device:TPU:1, one launch (start us, length us, event | category | flops | bytes accessed | tf_op | source)
XLA Modules:
  0.0 49.7 jit_solution(13684066641260655014)
XLA Ops:
  0.6 48.1 %krylov.1 = (f32[16,64]{1,0:T(8,128)S(1)}, f32[32,128]{1,0:T(8,128)S(1)}, f32[64,256]{1,0:T(8,128)S(1)}, f32[128,512]{1,0:T(8,128)S(1)}, f32[16,64]{1,0:T(8,128)...) custom-call(f32[8,8192]{1,0:T(8,128)} %refs_0_.1, ...), custom_call_target="tpu_custom_call" | custom-call | tf_op jit(solution)/shard_map/krylov/pallas_call | solution.py:423
  48.7 0.9 %combine.1 = (f32[16,64]{1,0:T(8,128)}, f32[32,128]{1,0:T(8,128)}, f32[64,256]{1,0:T(8,128)}, f32[128,512]{1,0:T(8,128)}, f32[8,8192]{1,0:T(8,128)}) custom-call(f32[1,128]{1,0:T(1,128)S(1)} %get-tuple-element.16.refs_0_, f32[16,64]{1,0:T(8,128)S(1)} %get-tuple-element.17.refs_1_, f32[32,128]{1,0:T(8,128)S(1)} %get-tuple-element.18.refs_2_, ...), custom_call_target="tpu_custom_call" | custom-call | tf_op jit(solution)/shard_map/combine/pallas_call | solution.py:461

commit v3 on v2

--- a/solution.py
+++ b/solution.py
@@ -51,7 +51,8 @@
     spread = np.zeros((rows, 128 * len(row_parts)))
     for k, part in enumerate(row_parts):
         spread[:, 128 * k : 128 * k + part.shape[0]] = part.T
-    return halves(back), halves(spread), halves(np.concatenate(col_parts, axis=1))
+    edges = [x for part in row_parts for x in (part[:8], part[-8:])]
+    return halves(back), halves(np.concatenate(edges)), halves(spread), halves(np.concatenate(col_parts, axis=1))
 
 
 def halve(x):
@@ -107,12 +108,14 @@
 
 def kernel(n_lat, n_lon, *refs):
     (
-        obs_hbm, gau_hbm, back_hbm, spread_hbm, cols_hbm,
+        obs_hbm, gau_hbm, back_hbm, edge_hbm, spread_hbm, cols_hbm,
         r0_out, r1_out, r2_out, r3_out, q0_out, q1_out, q2_out, q3_out, first_out, second_out, mix_out,
-        obs_ref, gau_ref, back, spread, table, obs_pad, obs_tile, gau_pad, gau_send, gau_recv, extended,
-        up_send, down_send, from_up, from_down, swath_src, swath_dst, red_src, red_plane, red_line,
-        load_sem, obs_sem, gau_sem, strip_sem, swath_sem, plane_sem, line_sem,
+        obs_ref, gau_ref, back, edge, spread, table, obs_pad, obs_tile, gau_pad, gau_send, gau_recv, extended,
+        part0, part1, part2, part3, right0, right1, right2, right3, surface_ref, mu_ref, strip_send, strip_recv, swath_src, swath_dst, red_src, red_plane, red_line,
+        load_sem, obs_sem, gau_sem, strip_sem, swath_sem, plane_sem, line_sem, line_ready,
     ) = refs
+    part_ref = (part0, part1, part2, part3)
+    right_ref = (right0, right1, right2, right3)
     r_out = (r0_out, r1_out, r2_out, r3_out)
     q_out = (q0_out, q1_out, q2_out, q3_out)
     lat, lon = lax.axis_index("lat"), lax.axis_index("lon")
@@ -130,39 +133,57 @@
     def lat_peer(d):
         return lax.rem(lat + d, n_lat)
 
+    twin = lat + 1 - 2 * lax.rem(lat, 2)
+
     def plane_peer(e):
-        twin = lat + 1 - 2 * lax.rem(lat, 2)
-        return {"lat": jnp.where(e >= n_lon, twin, lat), "lon": lon_peer(e)}
+        return {"lat": twin if e >= n_lon else lat, "lon": lon_peer(e)}
 
     def line_peer(f):
         return {"lat": lat_peer(2 * f)}
-
-    barrier = pltpu.get_barrier_semaphore()
-
-    def greet_line(f, c):
-        pl.semaphore_signal(barrier, inc=1, device_id=line_peer(f), device_id_type=MESH)
-        return c
-
-    def greet_plane(e, c):
-        pl.semaphore_signal(barrier, inc=1, device_id=plane_peer(e), device_id_type=MESH)
-        return c
-
-    beyond = {"lat": lax.rem(lat + n_lat - 1 + 2 * lax.rem(lat, 2), n_lat)}
-    lax.fori_loop(1, n_lat // 2, greet_line, 0)
-    pl.semaphore_signal(barrier, inc=1, device_id=beyond, device_id_type=MESH)
-    lax.fori_loop(1, 2 * n_lon, greet_plane, 0)
 
     loads = [
         pltpu.make_async_copy(src, dst, load_sem.at[i])
         for i, (src, dst) in enumerate(
-            ((obs_hbm, obs_ref), (gau_hbm, gau_ref), (back_hbm, back), (spread_hbm, spread), (cols_hbm, table))
+            (
+                (obs_hbm, obs_ref),
+                (gau_hbm, gau_ref),
+                (edge_hbm, edge),
+                (cols_hbm, table),
+                (back_hbm, back),
+                (spread_hbm, spread),
+            )
         )
     ]
     for load in loads:
         load.start()
+
+    valid = []
+    inside = []
+    for k, s in enumerate(SPACINGS):
+        row = lax.broadcasted_iota(jnp.int32, (heights[k], 1), 0) - MARGIN
+        col = lax.broadcasted_iota(jnp.int32, (1, lanes[k]), 1) - HALO // s
+        row_global, col_global = row + lat * (rows // s), col + lon * (cols // s)
+        row_ok = jnp.where((row_global >= 0) & (row_global < n_lat * (rows // s)), 1.0, 0.0)
+        col_ok = jnp.where((col_global >= 0) & (col_global < n_lon * (cols // s)), 1.0, 0.0)
+        valid.append(row_ok * col_ok)
+        inside.append(jnp.where((col >= 0) & (col < cols // s), 1.0, 0.0))
+
+    barrier = pltpu.get_barrier_semaphore()
+    beyond = {"lat": lax.rem(lat + n_lat - 1 + 2 * lax.rem(lat, 2), n_lat)}
+    planes = n_lat // 2
+    line = sorted(range(1, planes), key=lambda f: abs(f - planes // 2))
+    reach = max(planes // 4, 1)
+    near = [f for f in line if min(f, planes - f) <= reach]
+    plane = sorted(range(1, 2 * n_lon), key=lambda e: abs(e % n_lon - n_lon // 2))
+    for f in near:
+        pl.semaphore_signal(barrier, inc=1, device_id=line_peer(f), device_id_type=MESH)
+    for e in plane:
+        pl.semaphore_signal(barrier, inc=1, device_id=plane_peer(e), device_id_type=MESH)
+    pl.semaphore_signal(barrier, inc=1, device_id=beyond, device_id_type=MESH)
+
     extended[...] = jnp.zeros_like(extended)
-    for load in loads:
-        load.wait()
+    loads[0].wait()
+    loads[1].wait()
     obs_pad[:, :128] = jnp.zeros((swath, 128), F32)
     obs_pad[:, n_lon * cols :] = jnp.zeros((swath, 128), F32)
     obs_pad[:, HALO : HALO + n_lon * cols] = obs_ref[...]
@@ -176,7 +197,9 @@
     gau_send[0] = jnp.where(lane < HALO, roll(last[:half], HALO, 1), last[half:])
     gau_send[1] = jnp.where(lane < HALO, first[:half], roll(first[half:], HALO, 1))
 
-    pl.semaphore_wait(barrier, n_lat // 2 - 1 + 1 + 2 * n_lon - 1)
+    pl.semaphore_wait(barrier, len(near) + 1 + 2 * n_lon - 1)
+    for f in (reach, planes - reach):
+        pl.semaphore_signal(line_ready, inc=1, device_id=line_peer(f), device_id_type=MESH)
 
     def scatter(d, c):
         peer = lon_peer(d)
@@ -207,6 +230,8 @@
     own = pl.ds(pl.multiple_of(lon * swath, 8), swath)
     obs_tile[own, :] = obs_pad[:, pl.ds(pl.multiple_of(lon * cols, 128), width)]
 
+    for load in loads[2:]:
+        load.wait()
     to_right.wait()
     to_left.wait()
     packed = gau_recv[0] * jnp.where(lon > 0, 1.0, 0.0)
@@ -219,26 +244,32 @@
     pltpu.make_async_copy(all_obs, all_obs, obs_sem.at[1]).wait()
     pltpu.make_async_copy(all_obs, all_obs, obs_sem.at[0]).wait()
 
-    valid = []
-    inside = []
-    for k, s in enumerate(SPACINGS):
-        row = lax.broadcasted_iota(jnp.int32, (heights[k], 1), 0) - MARGIN
-        col = lax.broadcasted_iota(jnp.int32, (1, lanes[k]), 1) - HALO // s
-        row_global, col_global = row + lat * (rows // s), col + lon * (cols // s)
-        row_ok = jnp.where((row_global >= 0) & (row_global < n_lat * (rows // s)), 1.0, 0.0)
-        col_ok = jnp.where((col_global >= 0) & (col_global < n_lon * (cols // s)), 1.0, 0.0)
-        valid.append(row_ok * col_ok)
-        inside.append(jnp.where((col >= 0) & (col < cols // s), 1.0, 0.0))
+    row8 = lax.broadcasted_iota(jnp.int32, (8, 1), 0)
+    above = row8 >= MARGIN
+    summed = (row8 >= 2) & (row8 < 6)
+
+    def span(k):
+        return slice(starts[k], starts[k] + lanes[k])
 
     def adjoint(misfit):
         part = into(back[...], misfit)
-        result = []
         for k in range(3):
-            at = slice(starts[k], starts[k] + lanes[k])
-            result.append(times(part[tops[k] : tops[k] + heights[k]], table[:width, at], table[width:, at]))
+            rows_k = part[tops[k] : tops[k] + heights[k]]
+            part_ref[k][...] = times(rows_k, table[:width, span(k)], table[width:, span(k)])
         extended[MARGIN : MARGIN + rows, :] = five(misfit, 1)
-        result.append(five(extended[...], 0))
-        return result
+        part3[...] = five(extended[...], 0)
+
+    def adjoint_edges(misfit):
+        part = into(edge[...], misfit)
+        heads, tails = [], []
+        for k in range(3):
+            both = times(part[16 * k : 16 * k + 16], table[:width, span(k)], table[width:, span(k)])
+            heads.append(both[:8])
+            tails.append(both[8:])
+        near, away = five(misfit[:8], 1), five(misfit[rows - 8 :], 1)
+        heads.append(five(jnp.where(above, roll(near, 4, 0), 0.0), 0))
+        tails.append(five(jnp.where(above, 0.0, roll(away, 4, 0)), 0))
+        return heads, tails
 
     def forward(coeffs):
         parts = [into(spread[:, 128 * k : 128 * k + heights[k]], coeffs[k]) for k in range(3)]
@@ -246,17 +277,17 @@
         fine = five(coeffs[3], 0)[MARGIN : MARGIN + rows]
         return coarse + five(fine, 1)
 
-    def strips(which, partial):
-        for k in range(LEVELS):
-            at = slice(starts[k], starts[k] + lanes[k])
-            up_send[which, :, at] = partial[k][:8]
-            down_send[which, :, at] = partial[k][heights[k] - 8 :]
+    def strips(which, heads, tails):
         copies = []
-        for j, (src, dst, d) in enumerate(((up_send, from_down, n_lat - 1), (down_send, from_up, 1))):
+        for j, (tile, d) in enumerate(((heads, n_lat - 1), (tails, 1))):
+            coarse = roll(jnp.concatenate(tile[:3], axis=1), 2, 0)
+            fine = roll(tile[3], -2, 0)
+            strip_send[which, j, :, :width] = jnp.where(above, coarse[:, :width], fine)
+            strip_send[which, j, :, width:] = coarse[:, width:]
             copies.append(
                 pltpu.make_async_remote_copy(
-                    src_ref=src.at[which],
-                    dst_ref=dst.at[which],
+                    src_ref=strip_send.at[which, j],
+                    dst_ref=strip_recv.at[which, j],
                     send_sem=strip_sem.at[4 * which + 2 * j],
                     recv_sem=strip_sem.at[4 * which + 2 * j + 1],
                     device_id={"lat": lat_peer(d)},
@@ -266,15 +297,23 @@
             copies[-1].start()
         return copies
 
-    def joined(which, partial):
+    def received(which, j, has):
+        packed = strip_recv[which, j] * has
+        coarse = jnp.where(summed, roll(packed, -2, 0), 0.0)
+        fine = jnp.where(summed, roll(packed[:, :width], 2, 0), 0.0)
+        return [coarse[:, span(k)] for k in range(3)] + [fine]
+
+    def joined(which, extra=None):
+        above_it = received(which, 1, jnp.where(lat > 0, 1.0, 0.0))
+        below_it = received(which, 0, jnp.where(lat < n_lat - 1, 1.0, 0.0))
         result = []
-        has_up = jnp.where(lat > 0, 1.0, 0.0)
-        has_down = jnp.where(lat < n_lat - 1, 1.0, 0.0)
         for k in range(LEVELS):
-            at = slice(starts[k], starts[k] + lanes[k])
-            head = partial[k][:8] + has_up * from_up[which, :, at]
-            tail = partial[k][heights[k] - 8 :] + has_down * from_down[which, :, at]
-            middle = partial[k][8 : heights[k] - 8]
+            partial = part_ref[k][...]
+            if extra:
+                partial = partial + extra[k]
+            head = partial[:8] + above_it[k]
+            tail = partial[heights[k] - 8 :] + below_it[k]
+            middle = partial[8 : heights[k] - 8]
             result.append(jnp.concatenate([head, middle, tail], axis=0) * valid[k])
         return result
 
@@ -299,7 +338,6 @@
         s = SPACINGS[k]
         return x[MARGIN : MARGIN + rows // s, HALO // s : HALO // s + cols // s]
 
-    above = lax.broadcasted_iota(jnp.int32, (8, 1), 0) >= MARGIN
 
     def squares(k, x):
         y = x * x
@@ -314,29 +352,50 @@
         misfit = 2.0 * gau_pad[...] * surface
         return misfit, fold_lanes(fold(misfit * surface) * own_lane)
 
-    partial = adjoint(2.0 * gau_pad[...] * obs_tile[...])
-    copies = strips(0, partial)
+    misfit = 2.0 * gau_pad[...] * obs_tile[...]
+    copies = strips(0, *adjoint_edges(misfit))
+
+    @pl.when(lat >= 0)
+    def _():
+        adjoint(2.0 * gau_pad[...] * obs_tile[...])
+
     for copy in copies:
         copy.wait()
-    right = joined(0, partial)
+    right = joined(0)
 
     surface = forward(right)
-    misfit, mu1 = misfits(surface)
-    partial = adjoint(misfit)
-    copies = strips(1, partial)
-    swath_src[0] = surface[:, HALO : HALO + cols]
-    send_swaths(0)
-    mu0 = jnp.zeros((8, 128), F32)
-    rough = []
+    surface_ref[...] = surface
+    heads, tails = adjoint_edges(2.0 * gau_pad[...] * surface)
     for k in range(LEVELS):
-        smooth = stencil(right[k]) * valid[k]
-        rough.append(SCALES[k] * stencil(smooth) * valid[k])
-        mu0 = mu0 + squares(k, right[k])
-        mu1 = mu1 + SCALES[k] * squares(k, smooth)
-        r_out[k][...] = extract(k, right[k])
+        n = heights[k]
+        for tile, x, ok, own_rows in (
+            (heads, right[k][:8], valid[k][:8], above),
+            (tails, right[k][n - 8 :], valid[k][n - 8 :], ~above),
+        ):
+            tile[k] = tile[k] + SCALES[k] * stencil(stencil(jnp.where(own_rows, x, 0.0)) * ok)
+    copies = strips(1, heads, tails)
+    for k in range(LEVELS):
+        right_ref[k][...] = right[k]
+
+    @pl.when(lat >= 0)
+    def _():
+        misfit, mu1 = misfits(surface_ref[...])
+        adjoint(misfit)
+        mu0 = jnp.zeros((8, 128), F32)
+        for k in range(LEVELS):
+            x = right_ref[k][...]
+            n = heights[k]
+            head, tail = jnp.where(above, x[:8], 0.0), jnp.where(above, 0.0, x[n - 8 :])
+            own_x = jnp.concatenate([head, x[8 : n - 8], tail], axis=0)
+            part_ref[k][...] += SCALES[k] * stencil(stencil(own_x) * valid[k])
+            mu0 = mu0 + squares(k, x)
+            mu1 = mu1 + SCALES[k] * squares(k, stencil(x) * valid[k])
+        mu_ref[0] = mu0
+        mu_ref[1] = mu1
+
     for copy in copies:
         copy.wait()
-    image = [x + y for x, y in zip(joined(1, partial), rough)]
+    image = joined(1)
 
     surface = forward(image)
     mu2 = jnp.zeros((8, 128), F32)
@@ -345,13 +404,12 @@
         mu2 = mu2 + squares(k, image[k])
         mu3 = mu3 + SCALES[k] * squares(k, stencil(image[k]) * valid[k])
 
-    row8 = lax.broadcasted_iota(jnp.int32, (8, 128), 0)
+    sub8 = lax.broadcasted_iota(jnp.int32, (8, 128), 0)
     lane8 = lax.broadcasted_iota(jnp.int32, (8, 128), 1)
 
-    def reduce_start(stage, value, dst, sem, count, peer_of):
+    def reduce_start(stage, value, dst, sem, order, peer_of):
         red_src[stage] = value
-
-        def push(d, c):
+        for d in order:
             pltpu.make_async_remote_copy(
                 src_ref=red_src.at[stage],
                 dst_ref=dst.at[d - 1],
@@ -360,26 +418,31 @@
                 device_id=peer_of(d),
                 device_id_type=MESH,
             ).start()
-            return c
-
-        lax.fori_loop(1, count, push, 0)
 
     def reduce_end(value, dst, sem):
         pltpu.make_async_copy(dst, dst, sem.at[1]).wait()
         return value + jnp.sum(dst[...], axis=0)
 
     gathered = jnp.zeros((8, 128), F32)
-    for i, value in enumerate((mu0, mu1, mu2, mu3)):
-        gathered = gathered + jnp.where(row8 == i, jnp.sum(value, axis=0, keepdims=True), 0.0)
+    for i, value in enumerate((mu_ref[0], mu_ref[1], mu2, mu3)):
+        gathered = gathered + jnp.where(sub8 == i, jnp.sum(value, axis=0, keepdims=True), 0.0)
     gathered = jnp.sum(gathered, axis=1, keepdims=True)
-    moments = jnp.sum(jnp.where(row8 == lane8, gathered, 0.0), axis=0, keepdims=True)
-    reduce_start(0, moments, red_plane, plane_sem, 2 * n_lon, plane_peer)
+    moments = jnp.sum(jnp.where(sub8 == lane8, gathered, 0.0), axis=0, keepdims=True)
+    reduce_start(0, moments, red_plane, plane_sem, plane, plane_peer)
+    swath_src[0] = surface_ref[:, HALO : HALO + cols]
+    send_swaths(0)
     swath_src[1] = surface[:, HALO : HALO + cols]
     for k in range(LEVELS):
+        r_out[k][...] = extract(k, right_ref[k][...])
         q_out[k][...] = extract(k, image[k])
     moments = reduce_end(moments, red_plane, plane_sem)
-    reduce_start(1, moments, red_line, line_sem, n_lat // 2, line_peer)
+    pl.semaphore_wait(line_ready, 2)
+    reduce_start(1, moments, red_line, line_sem, line, line_peer)
     send_swaths(1)
+    everything = swath_dst.at[0, :, : (n_lon - 1) * cols]
+    for which, out in ((0, first_out), (1, second_out)):
+        pltpu.make_async_copy(everything, everything, swath_sem.at[2 * which + 1]).wait()
+        out[...] = swath_dst[which]
     moments = reduce_end(moments, red_line, line_sem)
 
     m0, m1, m2, m3 = (moments[:, i : i + 1] for i in range(4))
@@ -391,13 +454,10 @@
     lane1 = lane8[:1]
     mix_out[...] = jnp.where(lane1 == 0, alpha + gamma * grow, 0.0) + jnp.where(lane1 == 1, -alpha * gamma, 0.0)
 
-    everything = swath_dst.at[0, :, : (n_lon - 1) * cols]
-    for i in range(4):
-        pltpu.make_async_copy(everything, everything, swath_sem.at[i]).wait()
+    for which in range(2):
+        pltpu.make_async_copy(everything, everything, swath_sem.at[2 * which]).wait()
     pltpu.make_async_copy(red_plane, red_plane, plane_sem.at[0]).wait()
     pltpu.make_async_copy(red_line, red_line, line_sem.at[0]).wait()
-    first_out[...] = swath_dst[0]
-    second_out[...] = swath_dst[1]
 
 
 def combine(*refs):
@@ -413,10 +473,10 @@
     rows, cols = gauged.shape
     swath = observed.shape[0]
     width = cols + 2 * HALO
-    back, spread, table = tables(rows, cols)
+    back, edge, spread, table = tables(rows, cols)
     level_shapes = [jax.ShapeDtypeStruct((rows // s, cols // s), F32) for s in SPACINGS]
     swath_shape = jax.ShapeDtypeStruct(observed.shape, F32)
-    strip = 8 * sum(lanes_of(width, s) for s in SPACINGS)
+    node_shapes = [pltpu.VMEM((rows // s + 2 * MARGIN, lanes_of(width, s)), F32) for s in SPACINGS]
     vmem = pl.BlockSpec(memory_space=pltpu.VMEM)
     anywhere = pl.BlockSpec(memory_space=pl.ANY)
     dma = pltpu.SemaphoreType.DMA
@@ -424,12 +484,13 @@
         functools.partial(kernel, n_lat, n_lon),
         out_shape=[pltpu.VMEM(x.shape, F32) for x in (*level_shapes, *level_shapes, swath_shape, swath_shape)]
         + [pltpu.VMEM((1, 128), F32)],
-        in_specs=[anywhere] * 5,
+        in_specs=[anywhere] * 6,
         out_specs=[vmem] * 11,
         scratch_shapes=[
             pltpu.VMEM(observed.shape, F32),
             pltpu.VMEM(gauged.shape, gauged.dtype),
             pltpu.VMEM(back.shape, BF16),
+            pltpu.VMEM(edge.shape, BF16),
             pltpu.VMEM(spread.shape, BF16),
             pltpu.VMEM(table.shape, BF16),
             pltpu.VMEM((swath, n_lon * cols + 2 * HALO), F32),
@@ -438,23 +499,28 @@
             pltpu.VMEM((2, rows // 2, 128), F32),
             pltpu.VMEM((2, rows // 2, 128), F32),
             pltpu.VMEM((rows + 2 * MARGIN, width), F32),
-            *[pltpu.VMEM((2, 8, strip // 8), F32)] * 4,
+            *node_shapes,
+            *node_shapes,
+            pltpu.VMEM((rows, width), F32),
+            pltpu.VMEM((2, 8, 128), F32),
+            *[pltpu.VMEM((2, 2, 8, sum(lanes_of(width, s) for s in SPACINGS[:3])), F32)] * 2,
             pltpu.VMEM((2, rows, cols), F32),
             pltpu.VMEM((2, swath, n_lon * cols), F32),
             pltpu.VMEM((2, 1, 128), F32),
             pltpu.VMEM((2 * n_lon - 1, 1, 128), F32),
             pltpu.VMEM((n_lat // 2 - 1, 1, 128), F32),
-            dma((5,)),
+            dma((6,)),
             dma((2,)),
             dma((4,)),
             dma((8,)),
             dma((4,)),
             dma((2,)),
             dma((2,)),
+            pltpu.SemaphoreType.REGULAR,
         ],
         compiler_params=pltpu.CompilerParams(collective_id=0, has_side_effects=True),
         name="krylov",
-    )(observed, gauged, back, spread, table)
+    )(observed, gauged, back, edge, spread, table)
     mix, *pieces = [pltpu.with_memory_space_constraint(x, pltpu.VMEM) for x in (mix, *pieces)]
     firsts = [*pieces[:LEVELS], pieces[2 * LEVELS]]
     seconds = [*pieces[LEVELS : 2 * LEVELS], pieces[2 * LEVELS + 1]]

time: 49.8 us -> 47.3 us (0.950)
  Pallas kernels: 49 us -> 46.5 us
    pallas_call x1, Pallas kernels: 48.1 us -> 45.6 us  [body(): pl.pallas_call(functools.partial(kernel, n_lat, n_lon), out_shape=[pltpu....]
where the time goes in v3:
time: 47.3 us; the launch traced here: 47.1 us
  Pallas kernels  46.5 us (98%)
  between operations  0.64 us (1%)
    pallas_call x1, Pallas kernels, body(): pl.pallas_call(functools.partial(kernel, n_lat, n_lon), out_shape=[pltpu....  45.6 us

profile of v3, /device:TPU:1, one launch (start us, length us, event | category | flops | bytes accessed | tf_op | source)
XLA Modules:
  0.0 47.1 jit_solution(12630887581178955751)
XLA Ops:
  0.6 45.6 %krylov.1 = (f32[16,64]{1,0:T(8,128)S(1)}, f32[32,128]{1,0:T(8,128)S(1)}, f32[64,256]{1,0:T(8,128)S(1)}, f32[128,512]{1,0:T(8,128)S(1)}, f32[16,64]{1,0:T(8,128)...) custom-call(f32[8,8192]{1,0:T(8,128)} %refs_0_.1, ...), custom_call_target="tpu_custom_call" | custom-call | tf_op jit(solution)/shard_map/krylov/pallas_call | solution.py:483
  46.2 0.9 %combine.1 = (f32[16,64]{1,0:T(8,128)}, f32[32,128]{1,0:T(8,128)}, f32[64,256]{1,0:T(8,128)}, f32[128,512]{1,0:T(8,128)}, f32[8,8192]{1,0:T(8,128)}) custom-call(f32[1,128]{1,0:T(1,128)S(1)} %get-tuple-element.16.refs_0_, f32[16,64]{1,0:T(8,128)S(1)} %get-tuple-element.17.refs_1_, f32[32,128]{1,0:T(8,128)S(1)} %get-tuple-element.18.refs_2_, ...), custom_call_target="tpu_custom_call" | custom-call | tf_op jit(solution)/shard_map/combine/pallas_call | solution.py:527

commit v4 on v3

--- a/solution.py
+++ b/solution.py
@@ -130,6 +130,15 @@
     def lon_peer(d):
         return lax.rem(lon + d, n_lon)
 
+    def lon_partner(e):
+        peer = lon
+        for b in (1, 2, 4, 8):
+            if e & b and b < n_lon:
+                peer = peer + b - 2 * b * lax.rem(lon // b, 2)
+        return peer
+
+    order = sorted(range(1, n_lon), key=lambda e: (-(e & 2), -(e & 12), e & 1))
+
     def lat_peer(d):
         return lax.rem(lat + d, n_lat)
 
@@ -201,8 +210,8 @@
     for f in (reach, planes - reach):
         pl.semaphore_signal(line_ready, inc=1, device_id=line_peer(f), device_id_type=MESH)
 
-    def scatter(d, c):
-        peer = lon_peer(d)
+    def scatter(e):
+        peer = lon_partner(e)
         pltpu.make_async_remote_copy(
             src_ref=obs_pad.at[:, pl.ds(pl.multiple_of(peer * cols, 128), width)],
             dst_ref=obs_tile.at[pl.ds(pl.multiple_of(lon * swath, 8), swath), :],
@@ -211,7 +220,6 @@
             device_id={"lon": peer},
             device_id_type=MESH,
         ).start()
-        return c
 
     def beside(which, d):
         return pltpu.make_async_remote_copy(
@@ -224,7 +232,8 @@
         )
 
     to_right, to_left = beside(0, 1), beside(1, n_lon - 1)
-    lax.fori_loop(1, n_lon, scatter, 0)
+    for e in order:
+        scatter(e)
     to_right.start()
     to_left.start()
     own = pl.ds(pl.multiple_of(lon * swath, 8), swath)
@@ -318,8 +327,8 @@
         return result
 
     def send_swaths(which):
-        def push(d, c):
-            peer = lon_peer(d)
+        for e in order:
+            peer = lon_partner(e)
             pltpu.make_async_remote_copy(
                 src_ref=swath_src.at[which, pl.ds(pl.multiple_of(peer * swath, 8), swath), :],
                 dst_ref=swath_dst.at[which, :, pl.ds(pl.multiple_of(lon * cols, 128), cols)],
@@ -328,9 +337,6 @@
                 device_id={"lon": peer},
                 device_id_type=MESH,
             ).start()
-            return c
-
-        lax.fori_loop(1, n_lon, push, 0)
         at = pl.ds(pl.multiple_of(lon * cols, 128), cols)
         swath_dst[which, :, at] = swath_src[which, own, :]
 

time: 47.3 us -> 45.8 us (0.968)
  Pallas kernels: 46.5 us -> 45 us
    pallas_call x1, Pallas kernels: 45.6 us -> 44.1 us  [body(): pl.pallas_call(functools.partial(kernel, n_lat, n_lon), out_shape=[pltpu....]
where the time goes in v4:
time: 45.8 us; the launch traced here: 45.6 us
  Pallas kernels  45 us (98%)
  between operations  0.64 us (1%)
    pallas_call x1, Pallas kernels, body(): pl.pallas_call(functools.partial(kernel, n_lat, n_lon), out_shape=[pltpu....  44.1 us
    pallas_call x1, Pallas kernels, body(): pl.pallas_call(combine, out_shape=(*level_shapes, swath_shape), in_specs=...  0.94 us

profile of v4, /device:TPU:1, one launch (start us, length us, event | category | flops | bytes accessed | tf_op | source)
XLA Modules:
  0.0 45.6 jit_solution(5796272985269346534)
XLA Ops:
  0.6 44.1 %krylov.1 = (f32[16,64]{1,0:T(8,128)S(1)}, f32[32,128]{1,0:T(8,128)S(1)}, f32[64,256]{1,0:T(8,128)S(1)}, f32[128,512]{1,0:T(8,128)S(1)}, f32[16,64]{1,0:T(8,128)...) custom-call(f32[8,8192]{1,0:T(8,128)} %refs_0_.1, ...), custom_call_target="tpu_custom_call" | custom-call | tf_op jit(solution)/shard_map/krylov/pallas_call | solution.py:489
  44.7 0.9 %combine.1 = (f32[16,64]{1,0:T(8,128)}, f32[32,128]{1,0:T(8,128)}, f32[64,256]{1,0:T(8,128)}, f32[128,512]{1,0:T(8,128)}, f32[8,8192]{1,0:T(8,128)}) custom-call(f32[1,128]{1,0:T(1,128)S(1)} %get-tuple-element.16.refs_0_, f32[16,64]{1,0:T(8,128)S(1)} %get-tuple-element.17.refs_1_, f32[32,128]{1,0:T(8,128)S(1)} %get-tuple-element.18.refs_2_, ...), custom_call_target="tpu_custom_call" | custom-call | tf_op jit(solution)/shard_map/combine/pallas_call | solution.py:533

commit v5 on v4

--- a/solution.py
+++ b/solution.py
@@ -221,6 +221,28 @@
             device_id_type=MESH,
         ).start()
 
+    def finish(copy, sends, gets):
+        pl.when(sends)(lambda: copy.wait_send())
+        pl.when(gets)(lambda: copy.wait_recv())
+
+    has_up, has_down = lat > 0, lat < n_lat - 1
+
+    @pl.when(lon == 0)
+    def _():
+        gau_recv[0] = jnp.zeros_like(gau_recv[0])
+
+    @pl.when(lon == n_lon - 1)
+    def _():
+        gau_recv[1] = jnp.zeros_like(gau_recv[1])
+
+    @pl.when(lat == 0)
+    def _():
+        strip_recv[:, 1] = jnp.zeros_like(strip_recv[:, 1])
+
+    @pl.when(lat == n_lat - 1)
+    def _():
+        strip_recv[:, 0] = jnp.zeros_like(strip_recv[:, 0])
+
     def beside(which, d):
         return pltpu.make_async_remote_copy(
             src_ref=gau_send.at[which],
@@ -231,22 +253,23 @@
             device_id_type=MESH,
         )
 
+    has_left, has_right = lon > 0, lon < n_lon - 1
     to_right, to_left = beside(0, 1), beside(1, n_lon - 1)
     for e in order:
         scatter(e)
-    to_right.start()
-    to_left.start()
+    pl.when(has_right)(lambda: to_right.start())
+    pl.when(has_left)(lambda: to_left.start())
     own = pl.ds(pl.multiple_of(lon * swath, 8), swath)
     obs_tile[own, :] = obs_pad[:, pl.ds(pl.multiple_of(lon * cols, 128), width)]
 
     for load in loads[2:]:
         load.wait()
-    to_right.wait()
-    to_left.wait()
-    packed = gau_recv[0] * jnp.where(lon > 0, 1.0, 0.0)
+    finish(to_right, has_right, has_left)
+    finish(to_left, has_left, has_right)
+    packed = gau_recv[0]
     gau_pad[:half, :128] = jnp.where(lane < HALO, packed, gau_pad[:half, :128])
     gau_pad[half:, :128] = jnp.where(lane < HALO, roll(packed, HALO, 1), gau_pad[half:, :128])
-    packed = gau_recv[1] * jnp.where(lon < n_lon - 1, 1.0, 0.0)
+    packed = gau_recv[1]
     gau_pad[:half, cols:] = jnp.where(lane < HALO, gau_pad[:half, cols:], roll(packed, HALO, 1))
     gau_pad[half:, cols:] = jnp.where(lane < HALO, gau_pad[half:, cols:], packed)
     all_obs = obs_tile.at[: (n_lon - 1) * swath]
@@ -288,33 +311,35 @@
 
     def strips(which, heads, tails):
         copies = []
-        for j, (tile, d) in enumerate(((heads, n_lat - 1), (tails, 1))):
+        for j, (tile, d, sends, gets) in enumerate(
+            ((heads, n_lat - 1, has_up, has_down), (tails, 1, has_down, has_up))
+        ):
             coarse = roll(jnp.concatenate(tile[:3], axis=1), 2, 0)
             fine = roll(tile[3], -2, 0)
             strip_send[which, j, :, :width] = jnp.where(above, coarse[:, :width], fine)
             strip_send[which, j, :, width:] = coarse[:, width:]
-            copies.append(
-                pltpu.make_async_remote_copy(
-                    src_ref=strip_send.at[which, j],
-                    dst_ref=strip_recv.at[which, j],
-                    send_sem=strip_sem.at[4 * which + 2 * j],
-                    recv_sem=strip_sem.at[4 * which + 2 * j + 1],
-                    device_id={"lat": lat_peer(d)},
-                    device_id_type=MESH,
-                )
+            copy = pltpu.make_async_remote_copy(
+                src_ref=strip_send.at[which, j],
+                dst_ref=strip_recv.at[which, j],
+                send_sem=strip_sem.at[4 * which + 2 * j],
+                recv_sem=strip_sem.at[4 * which + 2 * j + 1],
+                device_id={"lat": lat_peer(d)},
+                device_id_type=MESH,
             )
-            copies[-1].start()
+            copies.append((copy, sends, gets))
+        for copy, sends, _ in copies:
+            pl.when(sends)(lambda: copy.start())
         return copies
 
-    def received(which, j, has):
-        packed = strip_recv[which, j] * has
+    def received(which, j):
+        packed = strip_recv[which, j]
         coarse = jnp.where(summed, roll(packed, -2, 0), 0.0)
         fine = jnp.where(summed, roll(packed[:, :width], 2, 0), 0.0)
         return [coarse[:, span(k)] for k in range(3)] + [fine]
 
     def joined(which, extra=None):
-        above_it = received(which, 1, jnp.where(lat > 0, 1.0, 0.0))
-        below_it = received(which, 0, jnp.where(lat < n_lat - 1, 1.0, 0.0))
+        above_it = received(which, 1)
+        below_it = received(which, 0)
         result = []
         for k in range(LEVELS):
             partial = part_ref[k][...]
@@ -366,7 +391,7 @@
         adjoint(2.0 * gau_pad[...] * obs_tile[...])
 
     for copy in copies:
-        copy.wait()
+        finish(*copy)
     right = joined(0)
 
     surface = forward(right)
@@ -400,7 +425,7 @@
         mu_ref[1] = mu1
 
     for copy in copies:
-        copy.wait()
+        finish(*copy)
     image = joined(1)
 
     surface = forward(image)

time: 45.8 us -> 45.7 us (level)
  no operation moved by 1% of the time
where the time goes in v5:
time: 45.7 us; the launch traced here: 45.6 us
  Pallas kernels  45 us (98%)
  between operations  0.64 us (1%)
    pallas_call x1, Pallas kernels, body(): pl.pallas_call(functools.partial(kernel, n_lat, n_lon), out_shape=[pltpu....  44 us
    pallas_call x1, Pallas kernels, body(): pl.pallas_call(combine, out_shape=(*level_shapes, swath_shape), in_specs=...  0.94 us

profile of v5, /device:TPU:1, one launch (start us, length us, event | category | flops | bytes accessed | tf_op | source)
XLA Modules:
  0.0 45.6 jit_solution(2744744990368077893)
XLA Ops:
  0.6 44.0 %krylov.1 = (f32[16,64]{1,0:T(8,128)S(1)}, f32[32,128]{1,0:T(8,128)S(1)}, f32[64,256]{1,0:T(8,128)S(1)}, f32[128,512]{1,0:T(8,128)S(1)}, f32[16,64]{1,0:T(8,128)...) custom-call(f32[8,8192]{1,0:T(8,128)} %refs_0_.1, ...), custom_call_target="tpu_custom_call" | custom-call | tf_op jit(solution)/shard_map/krylov/pallas_call | solution.py:514
  44.7 0.9 %combine.1 = (f32[16,64]{1,0:T(8,128)}, f32[32,128]{1,0:T(8,128)}, f32[64,256]{1,0:T(8,128)}, f32[128,512]{1,0:T(8,128)}, f32[8,8192]{1,0:T(8,128)}) custom-call(f32[1,128]{1,0:T(1,128)S(1)} %get-tuple-element.16.refs_0_, f32[16,64]{1,0:T(8,128)S(1)} %get-tuple-element.17.refs_1_, f32[32,128]{1,0:T(8,128)S(1)} %get-tuple-element.18.refs_2_, ...), custom_call_target="tpu_custom_call" | custom-call | tf_op jit(solution)/shard_map/combine/pallas_call | solution.py:558

commit v6 on v4

--- a/solution.py
+++ b/solution.py
@@ -387,16 +387,12 @@
     def _():
         misfit, mu1 = misfits(surface_ref[...])
         adjoint(misfit)
-        mu0 = jnp.zeros((8, 128), F32)
         for k in range(LEVELS):
             x = right_ref[k][...]
             n = heights[k]
             head, tail = jnp.where(above, x[:8], 0.0), jnp.where(above, 0.0, x[n - 8 :])
             own_x = jnp.concatenate([head, x[8 : n - 8], tail], axis=0)
             part_ref[k][...] += SCALES[k] * stencil(stencil(own_x) * valid[k])
-            mu0 = mu0 + squares(k, x)
-            mu1 = mu1 + SCALES[k] * squares(k, stencil(x) * valid[k])
-        mu_ref[0] = mu0
         mu_ref[1] = mu1
 
     for copy in copies:
@@ -404,9 +400,13 @@
     image = joined(1)
 
     surface = forward(image)
+    mu0, mu1 = jnp.zeros((8, 128), F32), mu_ref[1]
     mu2 = jnp.zeros((8, 128), F32)
     _, mu3 = misfits(surface)
     for k in range(LEVELS):
+        x = right_ref[k][...]
+        mu0 = mu0 + squares(k, x)
+        mu1 = mu1 + SCALES[k] * squares(k, stencil(x) * valid[k])
         mu2 = mu2 + squares(k, image[k])
         mu3 = mu3 + SCALES[k] * squares(k, stencil(image[k]) * valid[k])
 
@@ -430,7 +430,7 @@
         return value + jnp.sum(dst[...], axis=0)
 
     gathered = jnp.zeros((8, 128), F32)
-    for i, value in enumerate((mu_ref[0], mu_ref[1], mu2, mu3)):
+    for i, value in enumerate((mu0, mu1, mu2, mu3)):
         gathered = gathered + jnp.where(sub8 == i, jnp.sum(value, axis=0, keepdims=True), 0.0)
     gathered = jnp.sum(gathered, axis=1, keepdims=True)
     moments = jnp.sum(jnp.where(sub8 == lane8, gathered, 0.0), axis=0, keepdims=True)

time: 45.8 us -> 45.9 us (level)
  no operation moved by 1% of the time
where the time goes in v6:
time: 45.9 us; the launch traced here: 45.8 us
  Pallas kernels  45.2 us (98%)
  between operations  0.64 us (1%)
    pallas_call x1, Pallas kernels, body(): pl.pallas_call(functools.partial(kernel, n_lat, n_lon), out_shape=[pltpu....  44.2 us
    pallas_call x1, Pallas kernels, body(): pl.pallas_call(combine, out_shape=(*level_shapes, swath_shape), in_specs=...  0.94 us

profile of v6, /device:TPU:1, one launch (start us, length us, event | category | flops | bytes accessed | tf_op | source)
XLA Modules:
  0.0 45.8 jit_solution(1234332433824741102)
XLA Ops:
  0.6 44.2 %krylov.1 = (f32[16,64]{1,0:T(8,128)S(1)}, f32[32,128]{1,0:T(8,128)S(1)}, f32[64,256]{1,0:T(8,128)S(1)}, f32[128,512]{1,0:T(8,128)S(1)}, f32[16,64]{1,0:T(8,128)...) custom-call(f32[8,8192]{1,0:T(8,128)} %refs_0_.1, ...), custom_call_target="tpu_custom_call" | custom-call | tf_op jit(solution)/shard_map/krylov/pallas_call | solution.py:489
  44.9 0.9 %combine.1 = (f32[16,64]{1,0:T(8,128)}, f32[32,128]{1,0:T(8,128)}, f32[64,256]{1,0:T(8,128)}, f32[128,512]{1,0:T(8,128)}, f32[8,8192]{1,0:T(8,128)}) custom-call(f32[1,128]{1,0:T(1,128)S(1)} %get-tuple-element.16.refs_0_, f32[16,64]{1,0:T(8,128)S(1)} %get-tuple-element.17.refs_1_, f32[32,128]{1,0:T(8,128)S(1)} %get-tuple-element.18.refs_2_, ...), custom_call_target="tpu_custom_call" | custom-call | tf_op jit(solution)/shard_map/combine/pallas_call | solution.py:533
